TPU v7x, 512 devices: a whole 4x8x8 slice. The times are simulated.
512 devices in a mesh: snap: 32 (over x_hi, y, core), var: 16 (over z, x_lo).
Axes of the slice: x: 4 (x_hi: 2, x_lo: 2; x = x_hi * 2 + x_lo), y: 8, z: 8, core: 2. Of those that a mesh axis runs over, the one named last changes fastest.
Arguments:
- tensor: float32 [512, 1280, 1024], P('var', 'snap'), may hold values from 0.05 to 5
- cell_factor: float32 [1024, 256], P('snap'), may hold values from 0.1 to 1
- var_factor: float32 [512, 256], P('var'), may hold values from 0.1 to 1
- snap_factor: float32 [1280, 256], P('snap'), may hold values from 0.002 to 0.02
Outputs:
- grad_cells: float32 [1024, 256], P('snap')
- grad_vars: float32 [512, 256], P('var')
- grad_snaps: float32 [1280, 256], P('snap')
All inputs are finite; a program needn't handle non-finite values.
Results may differ from a plain program's by a relative error of at most 0.0003.
Values sent between devices are 32-bit elements; how exact they have to be, the bound alone decides.
No kernel may reach another device: no remote copies, remote signals or barrier semaphores. Data moves between devices by JAX's collectives and lax.ppermute only.
A program may use at most 64 MiB of HBM per device.

v0:
```python
import jax
import jax.numpy as jnp
from jax import lax
from jax.sharding import PartitionSpec as P

high = lax.Precision.HIGHEST


def local(tensor, cell_factor, var_factor, snap_factor):
    var_rows, snap_rows, cells = tensor.shape
    rank = cell_factor.shape[1]
    khatri = (var_factor[:, None, :] * snap_factor[None, :, :]).reshape(var_rows * snap_rows, rank)
    flat = tensor.reshape(var_rows * snap_rows, cells)
    all_cells = lax.all_gather(cell_factor, "snap", axis=0, tiled=True)
    model = jnp.dot(khatri, all_cells.T, precision=high, preferred_element_type=jnp.float32)
    deriv = (model - flat) * lax.rsqrt(model)
    partial_cells = jnp.dot(deriv.T, khatri, precision=high, preferred_element_type=jnp.float32)
    folded = jnp.dot(deriv, all_cells, precision=high, preferred_element_type=jnp.float32).reshape(
        var_rows, snap_rows, rank
    )
    partial_vars = jnp.einsum("vsr,sr->vr", folded, snap_factor, precision=high)
    partial_snaps = jnp.einsum("vsr,vr->sr", folded, var_factor, precision=high)
    summed = lax.psum(partial_cells, "var")
    grad_cells = lax.psum_scatter(summed, "snap", scatter_dimension=0, tiled=True)
    grad_vars = lax.psum(partial_vars, "snap")
    grad_snaps = lax.psum(partial_snaps, "var")
    return (grad_cells, grad_vars, grad_snaps)


def solution(mesh):
    placed = (P("var", "snap", None), P("snap", None), P("var", None), P("snap", None))
    return jax.shard_map(
        local,
        mesh=mesh,
        in_specs=placed,
        out_specs=(P("snap", None), P("var", None), P("snap", None)),
        check_vma=False,
    )
```

profile of v0, /device:TPU:6, one launch (start us, length us, event | category | flops | bytes accessed | tf_op | source)
XLA Modules:
  0.0 389.5 jit_solution(5850247747479945227)
XLA Ops:
  7.2 0.0 all-gather.2.cloned.1.call-start
  7.2 0.7 all-gather.2.cloned.1.call-update
  7.9 0.0 reduce-scatter.2.cloned.1.call-start
  7.9 0.9 broadcast_multiply_fusion
  8.8 88.6 %all-gather.2.cloned.1.call-done = f32[1024,256]{1,0:T(8,128)} async-done(((f32[32,256]{1,0:T(8,128)}), f32[1024,256]{1,0:T(8,128)}) %all-gather.2.cloned.1.call-update) | async-done | bytes 1048592 | tf_op jit(solution)/shard_map/all_gather | solution.py:14
  97.4 6.9 %fusion = f32[1280,1024]{1,0:T(8,128)S(1)} fusion(f32[32,40,1024]{2,1,0:T(8,128)} %param.4, f32[1280,256]{1,0:T(8,128)S(1)} %bitcast.20, f32[1024,256]{1,0:T(8,128)} %all-gather.2.cloned.1.call-done), kind=kOutput, calls=%fused_computation.1 | convolution fusion | flops 4029153280 | bytes 12845056 | tf_op jit(solution)/shard_map/dot_general | solution.py:15
  104.4 0.0 copy-start
  104.4 2.3 copy-done
  106.7 9.6 %fusion.1 = f32[1024,256]{1,0:T(8,128)} fusion(f32[1280,1024]{1,0:T(8,128)S(1)} %fusion, f32[1280,256]{1,0:T(8,128)S(1)} %bitcast.21), kind=kOutput, calls=%fused_computation.5 | convolution fusion | flops 4026531840 | bytes 7602176 | tf_op jit(solution)/shard_map/dot_general | solution.py:17
  116.2 0.0 copy-start.1
  116.2 0.0 reduce-scatter.2.cloned.1.call-update
  116.3 0.0 copy-start.3
  116.3 0.2 all-reduce.3.cloned.1.call-start
  116.5 1.0 copy-done.1
  117.5 6.2 %fusion.2 = f32[1280,256]{1,0:T(8,128)S(1)} fusion(f32[1280,1024]{1,0:T(8,128)} %copy-done, f32[1024,256]{1,0:T(8,128)S(1)} %copy-done.1), kind=kOutput, calls=%fused_computation.6 | convolution fusion | flops 4026531840 | bytes 7602176 | tf_op jit(solution)/shard_map/dot_general | solution.py:18
  123.7 0.0 copy-start.2
  123.7 0.0 copy-done.3
  123.7 0.7 multiply_reduce_fusion
  124.4 113.6 %reduce-scatter.2.cloned.1.call-done = f32[32,256]{1,0:T(8,128)} async-done(((f32[1024,256]{1,0:T(8,128)}), f32[32,256]{1,0:T(8,128)}) %reduce-scatter.2.cloned.1.call-update) | async-done | bytes 32784 | tf_op jit(solution)/shard_map/reduce_scatter | solution.py:24
  238.0 0.0 all-reduce.3.cloned.1.call-update
  238.1 0.0 copy-done.2
  238.1 0.1 multiply_reduce_fusion.1
  238.2 129.1 %psum.22 = f32[32,256]{1,0:T(8,128)} all-reduce(f32[32,256]{1,0:T(8,128)S(1)} %bitcast.27), channel_id=1, replica_groups=mesh['snap'=32,'var'=16] {'snap'}, use_global_device_ids=true, to_apply=%region_2.0 | all-reduce | flops 8192 | bytes 65536 | tf_op jit(solution)/shard_map/psum | solution.py:25
  367.3 12.8 %all-reduce.3.cloned.1.call-done = (f32[32,256]{1,0:T(8,128)}, f32[40,256]{1,0:T(8,128)}) async-done(((f32[32,256]{1,0:T(8,128)}, f32[40,256]{1,0:T(8,128)}), (f32[32,256]{1,0:T(8,128)}, f32[40,256]{1,0:T(8,128)})) %all-reduce.3.cloned.1.call-update) | async-done | bytes 73744 | tf_op jit(solution)/shard_map/psum | solution.py:23
  380.2 1.4 copy.23
  381.5 1.4 copy.24
Async XLA Ops:
  7.2 90.3 %all-gather.2.cloned.1.call-start = ((), (), s32[]{:S(2)}) async-start(), calls=%async_computation.1 | async-start | bytes 1081344 | tf_op jit(solution)/shard_map/all_gather | solution.py:14
  7.9 230.1 %reduce-scatter.2.cloned.1.call-start = ((), (), s32[]{:S(2)}) async-start(), calls=%async_computation.2 | async-start | bytes 1081344 | tf_op jit(solution)/shard_map/reduce_scatter | solution.py:24
  104.4 2.3 copy-start
  116.2 1.2 copy-start.1
  116.3 7.4 %copy-start.3 = (f32[32,256]{1,0:T(8,128)S(1)}, f32[32,256]{1,0:T(8,128)}, u32[]{:S(2)}) copy-start(f32[32,256]{1,0:T(8,128)} %param.6) | copy-start | bytes 98308
  116.3 263.9 %all-reduce.3.cloned.1.call-start = ((), (), s32[]{:S(2)}) async-start(), calls=%async_computation.3 | async-start | bytes 147456 | tf_op jit(solution)/shard_map/psum | solution.py:23
  123.7 114.4 %copy-start.2 = (f32[40,256]{1,0:T(8,128)S(1)}, f32[40,256]{1,0:T(8,128)}, u32[]{:S(2)}) copy-start(f32[40,256]{1,0:T(8,128)} %param.7) | copy-start | bytes 122884
Sparse Core Ops, SparseCore 0:
  11.3 86.0 all-gather.1
  116.4 121.6 reduce-scatter.1
  241.6 138.5 all-reduce.2
where the time goes:
time: 390 us; the launch traced here: 389 us
  waiting for transfers between devices  216 us (55%)
  blocking collectives  129 us (33%)
  matrix products  22.7 us (6%)
  between operations  13.8 us (4%)
  local copies, waits for them, and re-layouts  6.04 us (2%)
    psum x1, blocking collectives, local(): grad_vars = lax.psum(partial_vars, 'snap')  129 us
    reduce_scatter x1, waiting for transfers between devices, local(): lax.psum_scatter(summed, 'snap', scatter_dimension=0, tiled=True)  114 us
    all_gather x1, waiting for transfers between devices, local(): all_cells = lax.all_gather(cell_factor, 'snap', axis=0, tiled=True)  88.6 us
    psum x1, waiting for transfers between devices, local(): summed = lax.psum(partial_cells, 'var')  12.8 us
    dot_general x1, matrix products, local(): jnp.dot(deriv.T, khatri, precision=high, preferred_element_type=jnp.float32)  9.55 us
  transfers between devices with their start and end apart: 3, of which 3 were waited for; matrix products, arithmetic and copies ran while one was open for 2% of the time, Pallas kernels for 0%

commit v1 on v0

v1 whole, which is shorter than its diff:
```python
import jax
import jax.numpy as jnp
from jax import lax
from jax.sharding import Mesh, PartitionSpec as P

split3 = lax.Precision.HIGH
exact = lax.Precision.HIGHEST
snaps = ("xh", "y", "core")
rows = ("xh", "y")
variables = ("z", "xl")
swap = [(0, 1), (1, 0)]


def halves(a):
    lead = a.shape[:-2]
    a = a.reshape(*lead, a.shape[-2], 2, 128)
    return jnp.swapaxes(a, -3, -2).reshape(*lead, -1, 128)


def whole(a):
    n = a.shape[0] // 2
    return jnp.swapaxes(a.reshape(2, n, 128), 0, 1).reshape(n, 256)


def exchange(a, axes):
    return lax.all_to_all(a, axes, 0, 0)


def spread(a, axes, n):
    return exchange(jnp.broadcast_to(a[None], (n, *a.shape)), axes)


def local(tensor, cell_factor, var_factor, snap_factor):
    nv, ns, cells = tensor.shape
    own, rank = cell_factor.shape
    groups, peers = cells // own // 2, lax.axis_size(variables)
    core = lax.axis_index("core")
    khatri = (var_factor[:, None, :] * snap_factor[None, :, :]).reshape(nv * ns, rank)
    flat = tensor.reshape(nv * ns, cells)

    mine = spread(cell_factor, rows, groups)
    other = lax.ppermute(mine, "core", swap)
    first, second = jnp.where(core == 0, mine, other), jnp.where(core == 0, other, mine)
    all_cells = jnp.stack([first, second], axis=1).reshape(cells, rank)

    model = jnp.dot(khatri, all_cells.T, precision=split3, preferred_element_type=jnp.float32)
    deriv = (model - flat) * lax.rsqrt(model)
    folded = jnp.dot(deriv, all_cells, precision=split3, preferred_element_type=jnp.float32).reshape(nv, ns, rank)
    part_vars = jnp.einsum("vsr,sr->vr", folded, snap_factor, precision=exact)
    part_snaps = jnp.einsum("vsr,vr->sr", folded, var_factor, precision=exact)
    part_cells = jnp.dot(deriv.T, khatri, precision=split3, preferred_element_type=jnp.float32)
    part_cells = part_cells.reshape(groups, 2, own, rank)

    kept = lax.dynamic_index_in_dim(part_cells, core, 1, keepdims=False)
    given = lax.dynamic_index_in_dim(part_cells, 1 - core, 1, keepdims=False)
    kept = kept + lax.ppermute(given, "core", swap)
    part_vars = part_vars + lax.ppermute(part_vars, "core", swap)

    nc, nw = own * 2, nv * 2 // groups
    sent = jnp.concatenate([halves(kept), halves(part_vars).reshape(groups, nw, 128)], axis=1)
    got = exchange(sent, rows).sum(0)
    cell_sum, var_sum = got[:nc], got[nc:]
    sent = jnp.concatenate(
        [cell_sum.reshape(peers, -1, 128), halves(part_snaps).reshape(peers, -1, 128)], axis=1
    )
    got = exchange(sent, variables).sum(0)
    back = spread(got, variables, peers)
    k = nc // peers
    grad_cells = whole(back[:, :k].reshape(-1, 128))
    grad_snaps = whole(back[:, k:].reshape(-1, 128))
    grad_vars = whole(spread(var_sum, rows, groups).reshape(-1, 128))
    return grad_cells, grad_vars, grad_snaps


def solution(mesh):
    fine = Mesh(mesh.devices.reshape(2, 8, 2, 8, 2), ("xh", "y", "core", "z", "xl"))
    return jax.shard_map(
        local,
        mesh=fine,
        in_specs=(P(variables, snaps, None), P(snaps, None), P(variables, None), P(snaps, None)),
        out_specs=(P(snaps, None), P(variables, None), P(snaps, None)),
        check_vma=False,
    )
```

time: 390 us -> 133 us (0.34)
  the two profiles are of different devices: /device:TPU:6 before, /device:TPU:8 now
where the time goes in v1:
time: 133 us; the launch traced here: 132 us
  waiting for transfers between devices  47.6 us (36%)
  starting transfers between devices  32.6 us (25%)
  blocking collectives  26.1 us (20%)
  matrix products  12.1 us (9%)
  local copies, waits for them, and re-layouts  10.8 us (8%)
  other arithmetic  2.08 us (2%)
    all_to_all x4, waiting for transfers between devices, exchange(): return lax.all_to_all(a, axes, 0, 0)  44.6 us
    all_to_all x4, starting transfers between devices, exchange(): return lax.all_to_all(a, axes, 0, 0)  26.4 us
    all_to_all x1, blocking collectives, exchange(): return lax.all_to_all(a, axes, 0, 0)  26.1 us
    dot_general x1, local copies, waits for them, and re-layouts, local(): jnp.dot(deriv.T, khatri, precision=split3, preferred_element_type=jnp.flo...  5.94 us
    dot_general x1, matrix products, local(): jnp.dot(khatri, all_cells.T, precision=split3, preferred_element_type=jnp...  4.95 us
    dot_general x1, matrix products, local(): jnp.dot(deriv.T, khatri, precision=split3, preferred_element_type=jnp.flo...  4.85 us
  transfers between devices with their start and end apart: 7, of which 6 were waited for; matrix products, arithmetic and copies ran while one was open for 2% of the time, Pallas kernels for 0%

profile of v1, /device:TPU:8, one launch (start us, length us, event | category | flops | bytes accessed | tf_op | source)
XLA Modules:
  0.0 132.2 jit_solution(15833019855921079004)
XLA Ops:
  0.6 0.0 copy-start.3
  0.6 0.0 copy-start.2
  0.7 0.8 broadcast_in_dim.6
  1.5 26.1 %all_to_all.25 = f32[16,32,256]{2,1,0:T(8,128)S(1)} all-to-all(f32[16,32,256]{2,1,0:T(8,128)S(1)} %broadcast_in_dim.6), channel_id=1, replica_groups=mesh['xh'=2,'y'=8,'core'=2,'z'=8,'xl'=2] {'xh','y'}, dimensions={0} | all-to-all | bytes 1048576 | tf_op jit(solution)/shard_map/all_to_all | solution.py:26
  27.6 1.9 %collective-permute-start = (f32[16,32,256]{2,1,0:T(8,128)S(1)}, f32[16,32,256]{2,1,0:T(8,128)S(1)}, u32[]{:S(2)}, u32[]{:S(2)}) collective-permute-start(f32[16,32,256]{2,1,0:T(8,128)S(1)} %all_to_all.25), channel_id=1, source_target_pairs={{0,16},{16,0},{1,17},{17,1},{2,18},{18,2},{3,19},{19,3},{4,20},{20... | collective-permute-start | bytes 1572872 | tf_op jit(solution)/shard_map/ppermute | solution.py:42
  29.5 0.0 copy-done.3
  29.5 0.0 copy-done.2
  29.5 0.0 copy-start.1
  29.6 0.1 broadcast_multiply_fusion
  29.7 1.7 %collective-permute-done = f32[16,32,256]{2,1,0:T(8,128)S(1)} collective-permute-done((f32[16,32,256]{2,1,0:T(8,128)S(1)}, f32[16,32,256]{2,1,0:T(8,128)S(1)}, u32[]{:S(2)}, u32[]{:S(2)}) %collective-permute-start) | collective-permute-done | bytes 524320 | tf_op jit(solution)/shard_map/ppermute | solution.py:42
  31.4 0.1 select_bitcast_fusion.1
  31.5 0.1 pad_maximum_fusion
  31.6 0.5 copy-done.1
  32.0 5.0 %fusion = f32[1280,1024]{1,0:T(8,128)} fusion(f32[32,40,1024]{2,1,0:T(8,128)S(1)} %copy-done.1, f32[1280,256]{1,0:T(8,128)S(1)} %bitcast.69, f32[1024,256]{1,0:T(8,128)S(1)} %bitcast.71), kind=kOutput, calls=%fused_computation.1 | convolution fusion | flops 2015887360 | bytes 12845056 | tf_op jit(solution)/shard_map/dot_general | solution.py:46
  37.0 5.9 %copy.13 = f32[1024,1280]{1,0:T(8,128)} copy(f32[1024,1280]{0,1:T(8,128)} %bitcast.66) | data formatting | bytes 10485760 | tf_op jit(solution)/shard_map/dot_general | solution.py:51
  42.9 0.0 copy-start
  42.9 4.8 %fusion.1 = f32[16,2,32,256]{3,2,1,0:T(8,128)S(1)} fusion(f32[16,2,32,1280]{3,2,1,0:T(8,128)} %bitcast.68, f32[1280,256,1,1]{1,0,3,2:T(8,128)S(1)} %bitcast.70), kind=kOutput, calls=%fused_computation.16 | convolution fusion | flops 2013265920 | bytes 7602176 | tf_op jit(solution)/shard_map/dot_general | solution.py:51
  47.8 2.4 %collective-permute-start.1 = (f32[16,32,256]{2,1,0:T(8,128)S(1)}, f32[16,32,256]{2,1,0:T(8,128)S(1)}, u32[]{:S(2)}, u32[]{:S(2)}) collective-permute-start(f32[16,32,256]{2,1,0:T(8,128)S(1)} %dynamic-slice_bitcast_fusion), channel_id=1, source_target_pairs={{0,16},{16,0},{1,17},{17,1},{2,18},{18,2},{3,19},{19,3},{4,20},{20... | collective-permute-start | bytes 1572872 | tf_op jit(solution)/shard_map/ppermute | solution.py:56
  50.3 0.0 copy-done
  50.3 2.3 %multiply_reduce_fusion = (f32[256,40]{0,1:T(8,128)S(1)}, f32[32,40,256]{2,1,0:T(8,128)S(1)}) fusion(f32[256,32]{0,1:T(8,128)S(1)} %bitcast.78, f32[32,40,1024]{2,1,0:T(8,128)S(1)} %bitcast.67, f32[1024,256,1]{1,0,2:T(8,128)S(1)} %bitcast.72), kind=kOutput, calls=%fused_computation.2 | convolution fusion | flops 2013911040 | bytes 7675904 | tf_op jit(solution)/shard_map/dot_general | solution.py:48
  52.6 0.2 multiply_reduce_fusion.1
  52.7 1.9 %collective-permute-start.2 = (f32[32,256]{1,0:T(8,128)S(1)}, f32[32,256]{1,0:T(8,128)S(1)}, u32[]{:S(2)}, u32[]{:S(2)}) collective-permute-start(f32[32,256]{1,0:T(8,128)S(1)} %bitcast.79), channel_id=1, source_target_pairs={{0,16},{16,0},{1,17},{17,1},{2,18},{18,2},{3,19},{19,3},{4,20},{20... | collective-permute-start | bytes 98312 | tf_op jit(solution)/shard_map/ppermute | solution.py:57
  54.6 1.2 collective-permute-done.2
  55.9 0.0 collective-permute-done.1
  55.9 0.1 bitcast_add_fusion
  56.0 0.3 reshape.64
  56.2 0.1 copy.14
  56.3 0.9 pad_maximum_fusion.1
  57.2 5.4 %all-to-all-start.1 = ((f32[16,68,128]{2,1,0:T(8,128)}), f32[16,68,128]{2,1,0:T(8,128)S(1)}, u32[]{:S(2)}, u32[]{:S(2)}) async-start(f32[16,68,128]{2,1,0:T(8,128)} %pad_maximum_fusion.1), calls=%async_computation.1 | async-start | bytes 1179648 | tf_op jit(solution)/shard_map/all_to_all | solution.py:26
  62.7 17.1 %all-to-all-done.1 = f32[16,68,128]{2,1,0:T(8,128)S(1)} async-done(((f32[16,68,128]{2,1,0:T(8,128)}), f32[16,68,128]{2,1,0:T(8,128)S(1)}, u32[]{:S(2)}, u32[]{:S(2)}) %all-to-all-start.1) | async-done | bytes 557088 | tf_op jit(solution)/shard_map/all_to_all | solution.py:26
  79.9 0.7 pad_maximum_fusion.2
  80.5 10.4 %all-to-all-start.2 = ((f32[16,9,128]{2,1,0:T(8,128)}), f32[16,9,128]{2,1,0:T(8,128)S(1)}, u32[]{:S(2)}, u32[]{:S(2)}) async-start(f32[16,9,128]{2,1,0:T(8,128)} %pad_maximum_fusion.2), calls=%async_computation.2 | async-start | bytes 262144 | tf_op jit(solution)/shard_map/all_to_all | solution.py:26
  91.0 9.7 %all-to-all-done.2 = f32[16,9,128]{2,1,0:T(8,128)S(1)} async-done(((f32[16,9,128]{2,1,0:T(8,128)}), f32[16,9,128]{2,1,0:T(8,128)S(1)}, u32[]{:S(2)}, u32[]{:S(2)}) %all-to-all-start.2) | async-done | bytes 73760 | tf_op jit(solution)/shard_map/all_to_all | solution.py:26
  100.7 0.6 broadcast_in_dim.8
  101.3 7.0 %all-to-all-start.4 = ((f32[16,4,128]{2,1,0:T(4,128)}), f32[16,4,128]{2,1,0:T(4,128)S(1)}, u32[]{:S(2)}, u32[]{:S(2)}) async-start(f32[16,4,128]{2,1,0:T(4,128)} %broadcast_in_dim.8), calls=%async_computation.4 | async-start | bytes 65536 | tf_op jit(solution)/shard_map/all_to_all | solution.py:26
  108.3 8.7 %all-to-all-done.4 = f32[16,4,128]{2,1,0:T(4,128)S(1)} async-done(((f32[16,4,128]{2,1,0:T(4,128)}), f32[16,4,128]{2,1,0:T(4,128)S(1)}, u32[]{:S(2)}, u32[]{:S(2)}) %all-to-all-start.4) | async-done | bytes 32800 | tf_op jit(solution)/shard_map/all_to_all | solution.py:26
  117.0 0.7 broadcast_in_dim.7
  117.7 3.5 %all-to-all-start.3 = ((f32[16,9,128]{2,1,0:T(8,128)}), f32[16,9,128]{2,1,0:T(8,128)S(1)}, u32[]{:S(2)}, u32[]{:S(2)}) async-start(f32[16,9,128]{2,1,0:T(8,128)} %broadcast_in_dim.7), calls=%async_computation.3 | async-start | bytes 262144 | tf_op jit(solution)/shard_map/all_to_all | solution.py:26
  121.2 0.6 copy.41
  121.8 9.1 %all-to-all-done.3 = f32[16,9,128]{2,1,0:T(8,128)S(1)} async-done(((f32[16,9,128]{2,1,0:T(8,128)}), f32[16,9,128]{2,1,0:T(8,128)S(1)}, u32[]{:S(2)}, u32[]{:S(2)}) %all-to-all-start.3) | async-done | bytes 73760 | tf_op jit(solution)/shard_map/all_to_all | solution.py:26
  131.0 0.6 copy_bitcast_fusion
  131.6 0.6 copy.42
  (14 shorter events, 0.2 us)
Async XLA Ops:
  0.6 28.9 %copy-start.3 = (f32[32,256]{1,0:T(8,128)S(1)}, f32[32,256]{1,0:T(8,128)}, u32[]{:S(2)}) copy-start(f32[32,256]{1,0:T(8,128)} %param.6) | copy-start | bytes 98308
  0.6 28.9 %copy-start.2 = (f32[40,256]{1,0:T(8,128)S(1)}, f32[40,256]{1,0:T(8,128)}, u32[]{:S(2)}) copy-start(f32[40,256]{1,0:T(8,128)} %param.7) | copy-start | bytes 122884
  27.6 3.8 %collective-permute-start = (f32[16,32,256]{2,1,0:T(8,128)S(1)}, f32[16,32,256]{2,1,0:T(8,128)S(1)}, u32[]{:S(2)}, u32[]{:S(2)}) collective-permute-start(f32[16,32,256]{2,1,0:T(8,128)S(1)} %all_to_all.25), channel_id=1, source_target_pairs={{0,16},{16,0},{1,17},{17,1},{2,18},{18,2},{3,19},{19,3},{4,20},{20... | collective-permute-start | bytes 1572872 | tf_op jit(solution)/shard_map/ppermute | solution.py:42
  29.5 2.5 %copy-start.1 = (f32[32,40,1024]{2,1,0:T(8,128)S(1)}, f32[32,40,1024]{2,1,0:T(8,128)}, u32[]{:S(2)}) copy-start(f32[32,40,1024]{2,1,0:T(8,128)} %param.4) | copy-start | bytes 15728644
  42.9 7.3 %copy-start = (f32[1280,1024]{1,0:T(8,128)S(1)}, f32[1280,1024]{1,0:T(8,128)}, u32[]{:S(2)}) copy-start(f32[1280,1024]{1,0:T(8,128)} %fusion) | copy-start | bytes 15728644
  47.8 8.0 %collective-permute-start.1 = (f32[16,32,256]{2,1,0:T(8,128)S(1)}, f32[16,32,256]{2,1,0:T(8,128)S(1)}, u32[]{:S(2)}, u32[]{:S(2)}) collective-permute-start(f32[16,32,256]{2,1,0:T(8,128)S(1)} %dynamic-slice_bitcast_fusion), channel_id=1, source_target_pairs={{0,16},{16,0},{1,17},{17,1},{2,18},{18,2},{3,19},{19,3},{4,20},{20... | collective-permute-start | bytes 1572872 | tf_op jit(solution)/shard_map/ppermute | solution.py:56
  52.7 3.1 %collective-permute-start.2 = (f32[32,256]{1,0:T(8,128)S(1)}, f32[32,256]{1,0:T(8,128)S(1)}, u32[]{:S(2)}, u32[]{:S(2)}) collective-permute-start(f32[32,256]{1,0:T(8,128)S(1)} %bitcast.79), channel_id=1, source_target_pairs={{0,16},{16,0},{1,17},{17,1},{2,18},{18,2},{3,19},{19,3},{4,20},{20... | collective-permute-start | bytes 98312 | tf_op jit(solution)/shard_map/ppermute | solution.py:57
  57.2 22.6 %all-to-all-start.1 = ((f32[16,68,128]{2,1,0:T(8,128)}), f32[16,68,128]{2,1,0:T(8,128)S(1)}, u32[]{:S(2)}, u32[]{:S(2)}) async-start(f32[16,68,128]{2,1,0:T(8,128)} %pad_maximum_fusion.1), calls=%async_computation.1 | async-start | bytes 1179648 | tf_op jit(solution)/shard_map/all_to_all | solution.py:26
  80.5 20.1 %all-to-all-start.2 = ((f32[16,9,128]{2,1,0:T(8,128)}), f32[16,9,128]{2,1,0:T(8,128)S(1)}, u32[]{:S(2)}, u32[]{:S(2)}) async-start(f32[16,9,128]{2,1,0:T(8,128)} %pad_maximum_fusion.2), calls=%async_computation.2 | async-start | bytes 262144 | tf_op jit(solution)/shard_map/all_to_all | solution.py:26
  101.3 15.8 %all-to-all-start.4 = ((f32[16,4,128]{2,1,0:T(4,128)}), f32[16,4,128]{2,1,0:T(4,128)S(1)}, u32[]{:S(2)}, u32[]{:S(2)}) async-start(f32[16,4,128]{2,1,0:T(4,128)} %broadcast_in_dim.8), calls=%async_computation.4 | async-start | bytes 65536 | tf_op jit(solution)/shard_map/all_to_all | solution.py:26
  117.7 13.2 %all-to-all-start.3 = ((f32[16,9,128]{2,1,0:T(8,128)}), f32[16,9,128]{2,1,0:T(8,128)S(1)}, u32[]{:S(2)}, u32[]{:S(2)}) async-start(f32[16,9,128]{2,1,0:T(8,128)} %broadcast_in_dim.7), calls=%async_computation.3 | async-start | bytes 262144 | tf_op jit(solution)/shard_map/all_to_all | solution.py:26

commit v2 on v0

v2 whole, which is shorter than its diff:
```python
import jax
import jax.numpy as jnp
from jax import lax
from jax.experimental import pallas as pl
from jax.experimental.pallas import tpu as pltpu
from jax.sharding import Mesh, PartitionSpec as P

snaps = ("xh", "y", "core")
rows = ("xh", "y")
variables = ("z", "xl")
swap = [(0, 1), (1, 0)]
f32, bf16 = jnp.float32, jnp.bfloat16
lanes, frag, tile = 128, 32, 256
vmem = pl.BlockSpec(memory_space=pltpu.VMEM)
hbm = pl.BlockSpec(memory_space=pltpu.HBM)
small = pltpu.CompilerParams(vmem_limit_bytes=8 << 20)


def split(a):
    hi = a.astype(bf16)
    return hi, (a - hi.astype(f32)).astype(bf16)


def dot(a, b):
    return jnp.dot(a, b, preferred_element_type=f32)


def contract(core_ref, tensor_hbm, mine_ref, other_ref, var_hbm, snap_hbm, kept_ref, given_ref, snaps_ref,
             data, var_ref, snap_ref, cells, across, down, total, sems, small_sems):
    groups, own, rank = mine_ref.shape
    blocks, tiles, step, ns, _ = data.shape
    core = core_ref[0]
    loads = [
        [
            pltpu.make_async_copy(
                tensor_hbm.at[pl.ds(b * step, step), :, pl.ds(n * tile, tile)], data.at[b, n], sems.at[b, n]
            )
            for n in range(tiles)
        ]
        for b in range(blocks)
    ]
    factors = [
        pltpu.make_async_copy(snap_hbm, snap_ref, small_sems.at[0]),
        pltpu.make_async_copy(var_hbm, var_ref, small_sems.at[1]),
    ]
    for copy in factors + loads[0] + loads[1]:
        copy.start()
    for g in range(groups):
        cells[pl.ds(pl.multiple_of((2 * g + core) * own, own), own), :] = mine_ref[g]
        cells[pl.ds(pl.multiple_of((2 * g + 1 - core) * own, own), own), :] = other_ref[g]
    for n in range(tiles):
        block = cells[n * tile:(n + 1) * tile, :]
        hi, lo = split(block)
        down[n] = jnp.concatenate([hi, hi, lo], axis=0)
        hi, lo = split(block.T)
        across[n] = jnp.concatenate([hi, hi, lo], axis=0)
    for copy in factors:
        copy.wait()
    snap = snap_ref[...]
    snap_sum = jnp.zeros((ns, rank), f32)
    for b in range(blocks):
        var = var_ref[b * step:(b + 1) * step, :]
        khatri = (var[:, None, :] * snap[None, :, :]).reshape(step * ns, rank)
        hi, lo = split(khatri)
        k3 = jnp.concatenate([hi, lo, hi], axis=1)
        hi, lo = split(khatri.T)
        kt3 = jnp.concatenate([hi, lo, hi], axis=1)
        folded = jnp.zeros((step * ns, rank), f32)
        for n in range(tiles):
            model = dot(k3, across[n])
            loads[b][n].wait()
            hi, lo = split((model - data[b, n].reshape(step * ns, tile)) * lax.rsqrt(model))
            folded = folded + dot(jnp.concatenate([hi, lo, hi], axis=1), down[n])
            part = dot(kt3, jnp.concatenate([hi, hi, lo], axis=0))
            total[n] = part if b == 0 else total[n] + part
        folded = folded.reshape(step, ns, rank)
        sums = (folded * snap[None]).sum(1)
        kept_ref[groups, b * step:(b + 1) * step, :] = sums
        given_ref[groups, b * step:(b + 1) * step, :] = sums
        snap_sum = snap_sum + (folded * var[:, None, :]).sum(0)
    snaps_ref[...] = snap_sum
    for n in range(tiles):
        cells[n * tile:(n + 1) * tile, :] = total[n].T
    for g in range(groups):
        kept_ref[g] = cells[pl.ds(pl.multiple_of((2 * g + core) * own, own), own), :]
        given_ref[g] = cells[pl.ds(pl.multiple_of((2 * g + 1 - core) * own, own), own), :]


def contracted(core, tensor, mine, other, var, snap):
    groups, own, rank = mine.shape
    nv, ns, width = tensor.shape
    blocks, tiles = 2, width // tile
    halfsum = jax.ShapeDtypeStruct((groups + 1, own, rank), f32)
    return pl.pallas_call(
        contract,
        name="contract",
        in_specs=[pl.BlockSpec(memory_space=pltpu.SMEM), hbm, vmem, vmem, hbm, hbm],
        out_specs=[vmem] * 3,
        out_shape=[halfsum, halfsum, jax.ShapeDtypeStruct((ns, rank), f32)],
        scratch_shapes=[
            pltpu.VMEM((blocks, tiles, nv // blocks, ns, tile), f32),
            pltpu.VMEM((nv, rank), f32),
            pltpu.VMEM((ns, rank), f32),
            pltpu.VMEM((width, rank), f32),
            pltpu.VMEM((tiles, 3 * rank, tile), bf16),
            pltpu.VMEM((tiles, 3 * tile, rank), bf16),
            pltpu.VMEM((tiles, rank, tile), f32),
            pltpu.SemaphoreType.DMA((blocks, tiles)),
            pltpu.SemaphoreType.DMA((2,)),
        ],
        compiler_params=pltpu.CompilerParams(vmem_limit_bytes=36 << 20),
        cost_estimate=pl.CostEstimate(
            flops=18 * nv * ns * width * rank, bytes_accessed=4 * nv * ns * width, transcendentals=nv * ns * width
        ),
    )(core.reshape(1), tensor, mine, other, var, snap)


def turn(blocks):
    where = lax.broadcasted_iota(jnp.int32, blocks[0].shape, blocks[0].ndim - 1) // frag

    def pick(choices, at):
        out = choices[at(0)]
        for b in range(1, 4):
            out = jnp.where(where == b, choices[at(b)], out)
        return out

    shifted = []
    for s in range(4):
        y = pick(blocks, lambda b: (b + s) % 4)
        shifted.append(pltpu.roll(y, frag * s, y.ndim - 1) if s else y)
    return [pick(shifted, lambda b: (b - i) % 4) for i in range(4)]


def pack(kept_ref, got_ref, snaps_ref, out_ref):
    own, rank = kept_ref.shape[1:]
    ns = snaps_ref.shape[0]
    zero = jnp.zeros((own, lanes), f32)
    for h in range(rank // lanes):
        side = slice(h * lanes, (h + 1) * lanes)
        for u in range(5):
            if u < 4:
                blocks = [kept_ref[4 * i + u, :, side] + got_ref[4 * i + u, :, side] for i in range(4)]
            else:
                rest = jnp.concatenate([snaps_ref[own:, side], zero[: 2 * own - ns]], axis=0)
                blocks = [kept_ref[16, :, side] + got_ref[16, :, side], snaps_ref[:own, side], rest, zero]
            for i, block in enumerate(turn(blocks)):
                out_ref[pl.ds((4 * h + i) * own * 5 + u, own, stride=5), :] = block


def regroup(got_ref, out_ref):
    n = out_ref.shape[0]
    where = lax.broadcasted_iota(jnp.int32, (1, lanes), 1) // frag
    sums = []
    for u in range(4):
        sums.append(got_ref[pl.ds(u, n, stride=5), :].sum(0, keepdims=True))
    sums = jnp.concatenate(sums, axis=0)
    cells = [pltpu.roll(sums, frag * (3 - i), 1) if i < 3 else sums for i in range(4)]
    rest = got_ref[pl.ds(4, n, stride=5), :].reshape(16, n // 16, lanes)
    var, snap = rest.sum(0), rest.sum(1)
    by_group = jnp.where(where == 3, jnp.concatenate(cells, axis=0), snap)
    out = jnp.where(where[None] == 0, var[None], by_group[:, None, :])
    out_ref[...] = out.reshape(n, lanes)


def unpack(got_ref, cells_ref, var_ref, snap_ref):
    own = cells_ref.shape[0]
    ns = snap_ref.shape[0]
    for h in range(2):
        side = slice(h * lanes, (h + 1) * lanes)
        blocks = [got_ref[(4 * h + i) * own:(4 * h + i + 1) * own, :] for i in range(4)]
        var, first, rest, cells = turn(blocks)
        var_ref[:, side] = var
        snap_ref[:own, side] = first
        snap_ref[own:, side] = rest[: ns - own]
        cells_ref[:, side] = cells


def exchange(a, n):
    out = lax.all_to_all(a.reshape(n, -1, 1, lanes), rows + variables, 0, 0)
    return out.reshape(-1, lanes)


def local(tensor, cell_factor, var_factor, snap_factor):
    groups, peers = lax.axis_size(rows), lax.axis_size(variables)
    n = groups * peers
    mine = lax.all_to_all(jnp.broadcast_to(cell_factor[None], (groups, *cell_factor.shape)), rows, 0, 0)
    other = lax.ppermute(mine, "core", swap)
    kept, given, part_snaps = contracted(
        lax.axis_index("core"), tensor, mine, other, var_factor, snap_factor
    )
    got = lax.ppermute(given, "core", swap)
    sent = pl.pallas_call(
        pack, name="pack", in_specs=[vmem] * 3, out_specs=vmem,
        out_shape=jax.ShapeDtypeStruct((5 * n, lanes), f32), compiler_params=small,
    )(kept, got, part_snaps)
    sent = pl.pallas_call(
        regroup, name="regroup", in_specs=[vmem], out_specs=vmem,
        out_shape=jax.ShapeDtypeStruct((n, lanes), f32), compiler_params=small,
    )(exchange(sent, n))
    return pl.pallas_call(
        unpack, name="unpack", in_specs=[vmem], out_specs=[vmem] * 3,
        out_shape=[jax.ShapeDtypeStruct(a.shape, f32) for a in (cell_factor, var_factor, snap_factor)], compiler_params=small,
    )(exchange(sent, n))


def solution(mesh):
    fine = Mesh(mesh.devices.reshape(2, 8, 2, 8, 2), ("xh", "y", "core", "z", "xl"))
    return jax.shard_map(
        local,
        mesh=fine,
        in_specs=(P(variables, snaps, None), P(snaps, None), P(variables, None), P(snaps, None)),
        out_specs=(P(snaps, None), P(variables, None), P(snaps, None)),
        check_vma=False,
    )
```

time: 390 us -> 115 us (0.29)
  waiting for transfers between devices: 216 us -> 3.68 us
  blocking collectives: 129 us -> 87.4 us
  matrix products: 22.7 us -> 0 us
  between operations: 13.8 us -> 0.68 us
  Pallas kernels: 0 us -> 12.8 us
    psum x1 -> x0, blocking collectives: 129 us -> none  [local(): grad_vars = lax.psum(partial_vars, 'snap')]
    reduce_scatter x1 -> x0, waiting for transfers between devices: 114 us -> none  [local(): lax.psum_scatter(summed, 'snap', scatter_dimension=0, tiled=True)]
    all_gather x1 -> x0, waiting for transfers between devices: 88.6 us -> none  [local(): all_cells = lax.all_gather(cell_factor, 'snap', axis=0, tiled=True)]
    all_to_all x0 -> x3, blocking collectives: none -> 87.4 us  [the longest x2 63 us: exchange(): out = lax.all_to_all(a.reshape(n, -1, 1, lanes), rows + variables, 0, 0)]
    dot_general x3 -> x0, matrix products: 22.7 us -> none  [the longest x1 9.55 us: local(): jnp.dot(deriv.T, khatri, precision=high, preferred_element_type=jnp.float32)]
    pallas_call x0 -> x4, Pallas kernels: none -> 12.8 us  [the longest x1 11.8 us: contracted(): pl.pallas_call(contract, name='contract', in_specs=[pl.BlockSpec(memory_s...]
    psum x1 -> x0, waiting for transfers between devices: 12.8 us -> none  [local(): summed = lax.psum(partial_cells, 'var')]
    ppermute x0 -> x2, starting transfers between devices: none -> 3.95 us  [the longest x1 2.04 us: local(): got = lax.ppermute(given, 'core', swap)]
  transfers between devices with their start and end apart: 3 -> 2, of which waited for: 3 -> 2; matrix products, arithmetic and copies ran while one was open for 2% -> 0% of each run, Pallas kernels for 0% -> 0%
where the time goes in v2:
time: 115 us; the launch traced here: 113 us
  blocking collectives  87.4 us (76%)
  Pallas kernels  12.8 us (11%)
  local copies, waits for them, and re-layouts  4.82 us (4%)
  starting transfers between devices  3.95 us (3%)
  waiting for transfers between devices  3.68 us (3%)
    all_to_all x2, blocking collectives, exchange(): out = lax.all_to_all(a.reshape(n, -1, 1, lanes), rows + variables, 0, 0)  63 us
    all_to_all x1, blocking collectives, local(): lax.all_to_all(jnp.broadcast_to(cell_factor[None], (groups, *cell_factor....  24.4 us
    pallas_call x1, Pallas kernels, contracted(): pl.pallas_call(contract, name='contract', in_specs=[pl.BlockSpec(memory_s...  11.8 us
    unnamed x6, local copies, waits for them, and re-layouts  4.02 us
  transfers between devices with their start and end apart: 2, of which 2 were waited for; matrix products, arithmetic and copies ran while one was open for 0% of the time, Pallas kernels for 0%

profile of v2, /device:TPU:6, one launch (start us, length us, event | category | flops | bytes accessed | tf_op | source)
XLA Modules:
  0.0 113.3 jit_solution(14983813906316414554)
XLA Ops:
  0.6 0.8 broadcast_in_dim.2
  1.4 24.4 %all_to_all.15.mine_ref = f32[16,32,256]{2,1,0:T(8,128)S(1)} all-to-all(f32[16,32,256]{2,1,0:T(8,128)S(1)} %broadcast_in_dim.2), channel_id=1, replica_groups=mesh['xh'=2,'y'=8,'core'=2,'z'=8,'xl'=2] {'xh','y'}, dimensions={0} | all-to-all | bytes 1048576 | tf_op jit(solution)/shard_map/all_to_all | solution.py:186
  25.8 1.9 %collective-permute-start = (f32[16,32,256]{2,1,0:T(8,128)S(1)}, f32[16,32,256]{2,1,0:T(8,128)S(1)}, u32[]{:S(2)}, u32[]{:S(2)}) collective-permute-start(f32[16,32,256]{2,1,0:T(8,128)S(1)} %all_to_all.15.mine_ref), channel_id=1, source_target_pairs={{0,16},{16,0},{1,17},{17,1},{2,18},{18,2},{3,19},{19,3},{4,20},{20... | collective-permute-start | bytes 1572872 | tf_op jit(solution)/shard_map/ppermute | solution.py:187
  27.7 1.9 %collective-permute-done.other_ref = f32[16,32,256]{2,1,0:T(8,128)S(1)} collective-permute-done((f32[16,32,256]{2,1,0:T(8,128)S(1)}, f32[16,32,256]{2,1,0:T(8,128)S(1)}, u32[]{:S(2)}, u32[]{:S(2)}) %collective-permute-start) | collective-permute-done | bytes 524320 | tf_op jit(solution)/shard_map/ppermute | solution.py:187
  29.6 0.0 copy-start
  29.6 2.5 %copy-done = f32[32,40,1024]{2,1,0:T(8,128)S(1)} copy-done((f32[32,40,1024]{2,1,0:T(8,128)S(1)}, f32[32,40,1024]{2,1,0:T(8,128)}, u32[]{:S(2)}) %copy-start) | copy-done | bytes 5242904
  32.1 0.0 copy-start.1
  32.1 0.8 copy-done.1
  32.9 0.0 copy-start.2
  32.9 0.8 copy-done.2
  33.6 11.8 %contract.1 = (f32[17,32,256]{2,1,0:T(8,128)S(1)}, f32[17,32,256]{2,1,0:T(8,128)S(1)}, f32[40,256]{1,0:T(8,128)S(1)}) custom-call(s32[1]{0:T(128)} %bitcast.core_ref, f32[32,40,1024]{2,1,0:T(8,128)S(1)} %copy-done, f32[16,32,256]{2,1,0:T(8,128)S(1)} %all_to_all.15.mine_ref, f32[16,32,256]{2,1,0:T(8,128)S(1)} %collective-permute-done.other_ref, ...), custom_call_target="tpu_custom_call" | custom-call | flops 6039797760 | bytes 5242880 | tf_op jit(solution)/shard_map/contract/pallas_call | solution.py:94
  45.4 2.0 %collective-permute-start.1 = (f32[17,32,256]{2,1,0:T(8,128)S(1)}, f32[17,32,256]{2,1,0:T(8,128)S(1)}, u32[]{:S(2)}, u32[]{:S(2)}) collective-permute-start(f32[17,32,256]{2,1,0:T(8,128)S(1)} %get-tuple-element.7), channel_id=1, source_target_pairs={{0,16},{16,0},{1,17},{17,1},{2,18},{18,2},{3,19},{19,3},{4,20},{20... | collective-permute-start | bytes 1671176 | tf_op jit(solution)/shard_map/ppermute | solution.py:191
  47.4 1.8 %collective-permute-done.1.got_ref = f32[17,32,256]{2,1,0:T(8,128)S(1)} collective-permute-done((f32[17,32,256]{2,1,0:T(8,128)S(1)}, f32[17,32,256]{2,1,0:T(8,128)S(1)}, u32[]{:S(2)}, u32[]{:S(2)}) %collective-permute-start.1) | collective-permute-done | bytes 557088 | tf_op jit(solution)/shard_map/ppermute | solution.py:191
  49.2 0.2 pack.1
  49.4 40.7 %all_to_all.16 = f32[256,5,1,128]{3,2,1,0:T(1,128)S(1)} all-to-all(f32[256,5,1,128]{3,2,1,0:T(1,128)S(1)} %bitcast.7), channel_id=1, replica_groups=mesh['xh'=2,'y'=8,'core'=2,'z'=8,'xl'=2] {'xh','y','z','xl'}, dimensions={0} | all-to-all | bytes 1310720 | tf_op jit(solution)/shard_map/all_to_all | solution.py:179
  90.2 0.1 regroup.1
  90.3 22.3 %all_to_all.17 = f32[256,1,1,128]{3,2,1,0:T(1,128)S(1)} all-to-all(f32[256,1,1,128]{3,2,1,0:T(1,128)S(1)} %bitcast.10), channel_id=1, replica_groups=mesh['xh'=2,'y'=8,'core'=2,'z'=8,'xl'=2] {'xh','y','z','xl'}, dimensions={0} | all-to-all | bytes 262144 | tf_op jit(solution)/shard_map/all_to_all | solution.py:179
  112.6 0.7 unpack.1
Async XLA Ops:
  25.8 3.8 %collective-permute-start = (f32[16,32,256]{2,1,0:T(8,128)S(1)}, f32[16,32,256]{2,1,0:T(8,128)S(1)}, u32[]{:S(2)}, u32[]{:S(2)}) collective-permute-start(f32[16,32,256]{2,1,0:T(8,128)S(1)} %all_to_all.15.mine_ref), channel_id=1, source_target_pairs={{0,16},{16,0},{1,17},{17,1},{2,18},{18,2},{3,19},{19,3},{4,20},{20... | collective-permute-start | bytes 1572872 | tf_op jit(solution)/shard_map/ppermute | solution.py:187
  29.6 2.5 %copy-start = (f32[32,40,1024]{2,1,0:T(8,128)S(1)}, f32[32,40,1024]{2,1,0:T(8,128)}, u32[]{:S(2)}) copy-start(f32[32,40,1024]{2,1,0:T(8,128)} %tensor_hbm.1) | copy-start | bytes 15728644
  32.1 0.8 copy-start.1
  32.9 0.8 copy-start.2
  45.4 3.9 %collective-permute-start.1 = (f32[17,32,256]{2,1,0:T(8,128)S(1)}, f32[17,32,256]{2,1,0:T(8,128)S(1)}, u32[]{:S(2)}, u32[]{:S(2)}) collective-permute-start(f32[17,32,256]{2,1,0:T(8,128)S(1)} %get-tuple-element.7), channel_id=1, source_target_pairs={{0,16},{16,0},{1,17},{17,1},{2,18},{18,2},{3,19},{19,3},{4,20},{20... | collective-permute-start | bytes 1671176 | tf_op jit(solution)/shard_map/ppermute | solution.py:191

commit v3 on v2

--- a/solution.py
+++ b/solution.py
@@ -10,10 +10,14 @@
 variables = ("z", "xl")
 swap = [(0, 1), (1, 0)]
 f32, bf16 = jnp.float32, jnp.bfloat16
-lanes, frag, tile = 128, 32, 256
+lanes, frag, tile = 128, 64, 256
 vmem = pl.BlockSpec(memory_space=pltpu.VMEM)
 hbm = pl.BlockSpec(memory_space=pltpu.HBM)
 small = pltpu.CompilerParams(vmem_limit_bytes=8 << 20)
+
+
+def hold(a):
+    return pltpu.with_memory_space_constraint(a, pltpu.HBM)
 
 
 def split(a):
@@ -112,54 +116,52 @@
         cost_estimate=pl.CostEstimate(
             flops=18 * nv * ns * width * rank, bytes_accessed=4 * nv * ns * width, transcendentals=nv * ns * width
         ),
-    )(core.reshape(1), tensor, mine, other, var, snap)
-
-
-def turn(blocks):
-    where = lax.broadcasted_iota(jnp.int32, blocks[0].shape, blocks[0].ndim - 1) // frag
-
-    def pick(choices, at):
-        out = choices[at(0)]
-        for b in range(1, 4):
-            out = jnp.where(where == b, choices[at(b)], out)
-        return out
-
-    shifted = []
-    for s in range(4):
-        y = pick(blocks, lambda b: (b + s) % 4)
-        shifted.append(pltpu.roll(y, frag * s, y.ndim - 1) if s else y)
-    return [pick(shifted, lambda b: (b - i) % 4) for i in range(4)]
+    )(core, hold(tensor), mine, other, hold(var), hold(snap))
+
+
+def turn(a, b):
+    low = lax.broadcasted_iota(jnp.int32, a.shape, a.ndim - 1) < frag
+    axis = a.ndim - 1
+    return jnp.where(low, a, pltpu.roll(b, frag, axis)), jnp.where(low, pltpu.roll(a, frag, axis), b)
 
 
 def pack(kept_ref, got_ref, snaps_ref, out_ref):
     own, rank = kept_ref.shape[1:]
     ns = snaps_ref.shape[0]
+    n = out_ref.shape[0] // 6
     zero = jnp.zeros((own, lanes), f32)
+
+    def put(x, h, u, a, b):
+        for i, block in enumerate(turn(a, b)):
+            out_ref[pl.ds((x * n // 2 + (2 * h + i) * own) * 6 + u, own, stride=6), :] = block
+
     for h in range(rank // lanes):
         side = slice(h * lanes, (h + 1) * lanes)
-        for u in range(5):
-            if u < 4:
-                blocks = [kept_ref[4 * i + u, :, side] + got_ref[4 * i + u, :, side] for i in range(4)]
-            else:
-                rest = jnp.concatenate([snaps_ref[own:, side], zero[: 2 * own - ns]], axis=0)
-                blocks = [kept_ref[16, :, side] + got_ref[16, :, side], snaps_ref[:own, side], rest, zero]
-            for i, block in enumerate(turn(blocks)):
-                out_ref[pl.ds((4 * h + i) * own * 5 + u, own, stride=5), :] = block
-
-
-def regroup(got_ref, out_ref):
-    n = out_ref.shape[0]
-    where = lax.broadcasted_iota(jnp.int32, (1, lanes), 1) // frag
-    sums = []
-    for u in range(4):
-        sums.append(got_ref[pl.ds(u, n, stride=5), :].sum(0, keepdims=True))
-    sums = jnp.concatenate(sums, axis=0)
-    cells = [pltpu.roll(sums, frag * (3 - i), 1) if i < 3 else sums for i in range(4)]
-    rest = got_ref[pl.ds(4, n, stride=5), :].reshape(16, n // 16, lanes)
-    var, snap = rest.sum(0), rest.sum(1)
-    by_group = jnp.where(where == 3, jnp.concatenate(cells, axis=0), snap)
-    out = jnp.where(where[None] == 0, var[None], by_group[:, None, :])
-    out_ref[...] = out.reshape(n, lanes)
+        total = lambda g: kept_ref[g, :, side] + got_ref[g, :, side]
+        rest = jnp.concatenate([snaps_ref[own:, side], zero[: 2 * own - ns]], axis=0)
+        for x in range(2):
+            for u in range(4):
+                put(x, h, u, total(8 * x + u), total(8 * x + 4 + u))
+            put(x, h, 4, total(16), snaps_ref[:own, side])
+            put(x, h, 5, rest, zero)
+
+
+def regroup(x_ref, got_ref, out_ref):
+    n = got_ref.shape[0] // 6
+    low = lax.broadcasted_iota(jnp.int32, (1, lanes), 1) < frag
+    first = x_ref[1] == 0
+    unit = lambda u: got_ref[pl.ds(u, n, stride=6), :]
+    sums = jnp.concatenate([unit(u).sum(0, keepdims=True) for u in range(4)], axis=0)
+    cells = jnp.concatenate([pltpu.roll(sums, frag, 1), sums], axis=0)
+    mixed = unit(4).reshape(16, n // 16, lanes)
+    var, head = mixed.sum(0), mixed.sum(1)
+    rest = unit(5).reshape(16, n // 16, lanes).sum(1)
+    snap = jnp.where(low, rest, head)
+    snap = jnp.where(first, snap[:8], snap[8:])
+    shape = (8, n // 16, lanes)
+    out = jnp.where(low[None], var[None], cells[:, None, :])
+    out_ref[pl.ds(0, n // 2, stride=2), :] = out.reshape(n // 2, lanes)
+    out_ref[pl.ds(1, n // 2, stride=2), :] = jnp.broadcast_to(snap[:, None, :], shape).reshape(n // 2, lanes)
 
 
 def unpack(got_ref, cells_ref, var_ref, snap_ref):
@@ -167,17 +169,17 @@
     ns = snap_ref.shape[0]
     for h in range(2):
         side = slice(h * lanes, (h + 1) * lanes)
-        blocks = [got_ref[(4 * h + i) * own:(4 * h + i + 1) * own, :] for i in range(4)]
-        var, first, rest, cells = turn(blocks)
+        part = lambda i, u: got_ref[pl.ds(2 * (2 * h + i) * own + u, own, stride=2), :]
+        var, cells = turn(part(0, 0), part(1, 0))
+        rest, first = turn(part(0, 1), part(1, 1))
         var_ref[:, side] = var
         snap_ref[:own, side] = first
         snap_ref[own:, side] = rest[: ns - own]
         cells_ref[:, side] = cells
 
 
-def exchange(a, n):
-    out = lax.all_to_all(a.reshape(n, -1, 1, lanes), rows + variables, 0, 0)
-    return out.reshape(-1, lanes)
+def exchange(a, n, axes):
+    return lax.all_to_all(a.reshape(n, -1, 1, lanes), axes, 0, 0).reshape(-1, lanes)
 
 
 def local(tensor, cell_factor, var_factor, snap_factor):
@@ -185,22 +187,23 @@
     n = groups * peers
     mine = lax.all_to_all(jnp.broadcast_to(cell_factor[None], (groups, *cell_factor.shape)), rows, 0, 0)
     other = lax.ppermute(mine, "core", swap)
+    where = jnp.stack([lax.axis_index("core"), lax.axis_index("xh")])
     kept, given, part_snaps = contracted(
-        lax.axis_index("core"), tensor, mine, other, var_factor, snap_factor
+        where, tensor, mine, other, var_factor, snap_factor
     )
     got = lax.ppermute(given, "core", swap)
     sent = pl.pallas_call(
         pack, name="pack", in_specs=[vmem] * 3, out_specs=vmem,
-        out_shape=jax.ShapeDtypeStruct((5 * n, lanes), f32), compiler_params=small,
+        out_shape=jax.ShapeDtypeStruct((6 * n, lanes), f32), compiler_params=small,
     )(kept, got, part_snaps)
     sent = pl.pallas_call(
-        regroup, name="regroup", in_specs=[vmem], out_specs=vmem,
+        regroup, name="regroup", in_specs=[pl.BlockSpec(memory_space=pltpu.SMEM), vmem], out_specs=vmem,
         out_shape=jax.ShapeDtypeStruct((n, lanes), f32), compiler_params=small,
-    )(exchange(sent, n))
+    )(where, exchange(sent, n, rows + variables))
     return pl.pallas_call(
         unpack, name="unpack", in_specs=[vmem], out_specs=[vmem] * 3,
         out_shape=[jax.ShapeDtypeStruct(a.shape, f32) for a in (cell_factor, var_factor, snap_factor)], compiler_params=small,
-    )(exchange(sent, n))
+    )(exchange(sent, n // 2, ("y",) + variables))
 
 
 def solution(mesh):

time: 115 us -> 112 us (0.974)
  local copies, waits for them, and re-layouts: 4.82 us -> 0.8 us
  Pallas kernels: 12.8 us -> 15 us
    unnamed x6 -> x0, local copies, waits for them, and re-layouts: 4.02 us -> none
    pallas_call x1, Pallas kernels: 11.8 us -> 13.4 us  [contracted(): pl.pallas_call(contract, name='contract', in_specs=[pl.BlockSpec(memory_s...]
where the time goes in v3:
time: 112 us; the launch traced here: 110 us
  blocking collectives  86.4 us (77%)
  Pallas kernels  15 us (13%)
  starting transfers between devices  3.96 us (4%)
  waiting for transfers between devices  3.59 us (3%)
    all_to_all x2, blocking collectives, exchange(): lax.all_to_all(a.reshape(n, -1, 1, lanes), axes, 0, 0).reshape(-1, lanes)  62 us
    all_to_all x1, blocking collectives, local(): lax.all_to_all(jnp.broadcast_to(cell_factor[None], (groups, *cell_factor....  24.4 us
    pallas_call x1, Pallas kernels, contracted(): pl.pallas_call(contract, name='contract', in_specs=[pl.BlockSpec(memory_s...  13.4 us
  transfers between devices with their start and end apart: 2, of which 2 were waited for; matrix products, arithmetic and copies ran while one was open for 0% of the time, Pallas kernels for 0%

profile of v3, /device:TPU:6, one launch (start us, length us, event | category | flops | bytes accessed | tf_op | source)
XLA Modules:
  0.0 110.5 jit_solution(509400068629886639)
XLA Ops:
  0.6 0.8 broadcast_in_dim.2
  1.4 24.4 %all_to_all.15.mine_ref = f32[16,32,256]{2,1,0:T(8,128)S(1)} all-to-all(f32[16,32,256]{2,1,0:T(8,128)S(1)} %broadcast_in_dim.2), channel_id=1, replica_groups=mesh['xh'=2,'y'=8,'core'=2,'z'=8,'xl'=2] {'xh','y'}, dimensions={0} | all-to-all | bytes 1048576 | tf_op jit(solution)/shard_map/all_to_all | solution.py:188
  25.8 1.9 %collective-permute-start = (f32[16,32,256]{2,1,0:T(8,128)S(1)}, f32[16,32,256]{2,1,0:T(8,128)S(1)}, u32[]{:S(2)}, u32[]{:S(2)}) collective-permute-start(f32[16,32,256]{2,1,0:T(8,128)S(1)} %all_to_all.15.mine_ref), channel_id=1, source_target_pairs={{0,16},{16,0},{1,17},{17,1},{2,18},{18,2},{3,19},{19,3},{4,20},{20... | collective-permute-start | bytes 1572872 | tf_op jit(solution)/shard_map/ppermute | solution.py:189
  27.7 0.1 pad_add_fusion.core_ref.x_ref
  27.8 1.8 %collective-permute-done.other_ref = f32[16,32,256]{2,1,0:T(8,128)S(1)} collective-permute-done((f32[16,32,256]{2,1,0:T(8,128)S(1)}, f32[16,32,256]{2,1,0:T(8,128)S(1)}, u32[]{:S(2)}, u32[]{:S(2)}) %collective-permute-start) | collective-permute-done | bytes 524320 | tf_op jit(solution)/shard_map/ppermute | solution.py:189
  29.6 13.4 %contract.1 = (f32[17,32,256]{2,1,0:T(8,128)S(1)}, f32[17,32,256]{2,1,0:T(8,128)S(1)}, f32[40,256]{1,0:T(8,128)S(1)}) custom-call(s32[2]{0:T(128)S(1)} %pad_add_fusion.core_ref.x_ref, f32[32,40,1024]{2,1,0:T(8,128)} %tensor_hbm.1, f32[16,32,256]{2,1,0:T(8,128)S(1)} %all_to_all.15.mine_ref, f32[16,32,256]{2,1,0:T(8,128)S(1)} %collective-permute-done.other_ref, ...), custom_call_target="tpu_custom_call" | custom-call | flops 6039797760 | bytes 5242880 | tf_op jit(solution)/shard_map/contract/pallas_call | solution.py:98
  43.0 2.0 %collective-permute-start.1 = (f32[17,32,256]{2,1,0:T(8,128)S(1)}, f32[17,32,256]{2,1,0:T(8,128)S(1)}, u32[]{:S(2)}, u32[]{:S(2)}) collective-permute-start(f32[17,32,256]{2,1,0:T(8,128)S(1)} %get-tuple-element.7), channel_id=1, source_target_pairs={{0,16},{16,0},{1,17},{17,1},{2,18},{18,2},{3,19},{19,3},{4,20},{20... | collective-permute-start | bytes 1671176 | tf_op jit(solution)/shard_map/ppermute | solution.py:194
  45.1 1.8 %collective-permute-done.1.got_ref = f32[17,32,256]{2,1,0:T(8,128)S(1)} collective-permute-done((f32[17,32,256]{2,1,0:T(8,128)S(1)}, f32[17,32,256]{2,1,0:T(8,128)S(1)}, u32[]{:S(2)}, u32[]{:S(2)}) %collective-permute-start.1) | collective-permute-done | bytes 557088 | tf_op jit(solution)/shard_map/ppermute | solution.py:194
  46.9 0.2 pack.1
  47.1 43.3 %all_to_all.16 = f32[256,6,1,128]{3,2,1,0:T(1,128)S(1)} all-to-all(f32[256,6,1,128]{3,2,1,0:T(1,128)S(1)} %bitcast.9), channel_id=1, replica_groups=mesh['xh'=2,'y'=8,'core'=2,'z'=8,'xl'=2] {'xh','y','z','xl'}, dimensions={0} | all-to-all | bytes 1572864 | tf_op jit(solution)/shard_map/all_to_all | solution.py:182
  90.4 0.7 regroup.1
  91.1 18.7 %all_to_all.17 = f32[128,2,1,128]{3,1,2,0:T(2,128)S(1)} all-to-all(f32[128,2,1,128]{3,1,2,0:T(2,128)S(1)} %bitcast.10), channel_id=1, replica_groups=mesh['xh'=2,'y'=8,'core'=2,'z'=8,'xl'=2] {'y','z','xl'}, dimensions={0} | all-to-all | bytes 262144 | tf_op jit(solution)/shard_map/all_to_all | solution.py:182
  109.8 0.7 unpack.1
Async XLA Ops:
  25.8 3.8 %collective-permute-start = (f32[16,32,256]{2,1,0:T(8,128)S(1)}, f32[16,32,256]{2,1,0:T(8,128)S(1)}, u32[]{:S(2)}, u32[]{:S(2)}) collective-permute-start(f32[16,32,256]{2,1,0:T(8,128)S(1)} %all_to_all.15.mine_ref), channel_id=1, source_target_pairs={{0,16},{16,0},{1,17},{17,1},{2,18},{18,2},{3,19},{19,3},{4,20},{20... | collective-permute-start | bytes 1572872 | tf_op jit(solution)/shard_map/ppermute | solution.py:189
  43.0 3.9 %collective-permute-start.1 = (f32[17,32,256]{2,1,0:T(8,128)S(1)}, f32[17,32,256]{2,1,0:T(8,128)S(1)}, u32[]{:S(2)}, u32[]{:S(2)}) collective-permute-start(f32[17,32,256]{2,1,0:T(8,128)S(1)} %get-tuple-element.7), channel_id=1, source_target_pairs={{0,16},{16,0},{1,17},{17,1},{2,18},{18,2},{3,19},{19,3},{4,20},{20... | collective-permute-start | bytes 1671176 | tf_op jit(solution)/shard_map/ppermute | solution.py:194

commit v4 on v3

--- a/solution.py
+++ b/solution.py
@@ -29,94 +29,122 @@
     return jnp.dot(a, b, preferred_element_type=f32)
 
 
-def contract(core_ref, tensor_hbm, mine_ref, other_ref, var_hbm, snap_hbm, kept_ref, given_ref, snaps_ref,
-             data, var_ref, snap_ref, cells, across, down, total, sems, small_sems):
-    groups, own, rank = mine_ref.shape
-    blocks, tiles, step, ns, _ = data.shape
-    core = core_ref[0]
-    loads = [
-        [
-            pltpu.make_async_copy(
-                tensor_hbm.at[pl.ds(b * step, step), :, pl.ds(n * tile, tile)], data.at[b, n], sems.at[b, n]
-            )
-            for n in range(tiles)
-        ]
-        for b in range(blocks)
-    ]
+def prepare(tensor_hbm, var_hbm, snap_hbm, data_ref, khatri_ref, flipped_ref, var_ref, snap_ref, sems, small_sems):
+    blocks, n_rows, rank = khatri_ref.shape[0], khatri_ref.shape[1], khatri_ref.shape[2] // 2
+    step = data_ref.shape[0] // blocks
     factors = [
         pltpu.make_async_copy(snap_hbm, snap_ref, small_sems.at[0]),
         pltpu.make_async_copy(var_hbm, var_ref, small_sems.at[1]),
     ]
-    for copy in factors + loads[0] + loads[1]:
+    loads = [
+        pltpu.make_async_copy(tensor_hbm.at[pl.ds(b * step, step)], data_ref.at[pl.ds(b * step, step)], sems.at[b])
+        for b in range(blocks)
+    ]
+    for copy in factors + loads:
         copy.start()
-    for g in range(groups):
-        cells[pl.ds(pl.multiple_of((2 * g + core) * own, own), own), :] = mine_ref[g]
-        cells[pl.ds(pl.multiple_of((2 * g + 1 - core) * own, own), own), :] = other_ref[g]
-    for n in range(tiles):
-        block = cells[n * tile:(n + 1) * tile, :]
-        hi, lo = split(block)
-        down[n] = jnp.concatenate([hi, hi, lo], axis=0)
-        hi, lo = split(block.T)
-        across[n] = jnp.concatenate([hi, hi, lo], axis=0)
     for copy in factors:
         copy.wait()
-    snap = snap_ref[...]
+    for b in range(blocks):
+        khatri = var_ref[b * step:(b + 1) * step, :][:, None, :] * snap_ref[...][None, :, :]
+        khatri = khatri.reshape(n_rows, rank)
+        hi, lo = split(khatri)
+        khatri_ref[b, :, :rank] = hi
+        khatri_ref[b, :, rank:] = lo
+        hi, lo = split(khatri.T)
+        flipped_ref[b, :, :n_rows] = hi
+        flipped_ref[b, :, n_rows:] = lo
+    for copy in loads:
+        copy.wait()
+
+
+def prepared(tensor, var, snap):
+    nv, ns, width = tensor.shape
+    rank = var.shape[1]
+    blocks = 2
+    return pl.pallas_call(
+        prepare,
+        name="prepare",
+        in_specs=[hbm] * 3,
+        out_specs=[vmem] * 5,
+        out_shape=[
+            jax.ShapeDtypeStruct(tensor.shape, f32),
+            jax.ShapeDtypeStruct((blocks, nv * ns // blocks, 2 * rank), bf16),
+            jax.ShapeDtypeStruct((blocks, rank, 2 * nv * ns // blocks), bf16),
+            jax.ShapeDtypeStruct(var.shape, f32),
+            jax.ShapeDtypeStruct(snap.shape, f32),
+        ],
+        scratch_shapes=[pltpu.SemaphoreType.DMA((blocks,)), pltpu.SemaphoreType.DMA((2,))],
+        compiler_params=small,
+        cost_estimate=pl.CostEstimate(flops=0, bytes_accessed=8 * nv * ns * width, transcendentals=0),
+    )(hold(tensor), hold(var), hold(snap))
+
+
+def contract(where_ref, data_ref, khatri_ref, flipped_ref, var_ref, snap_ref, mine_ref, other_ref,
+             kept_ref, given_ref, snaps_ref, across, down, total):
+    groups, own, rank = mine_ref.shape
+    nv, ns, width = data_ref.shape
+    blocks, n_rows = khatri_ref.shape[:2]
+    tiles, step, per = width // tile, nv // blocks, tile // own // 2
+    even = where_ref[0] == 0
+
+    def sides(a, b):
+        return jnp.where(even, a, b), jnp.where(even, b, a)
+
     snap_sum = jnp.zeros((ns, rank), f32)
     for b in range(blocks):
-        var = var_ref[b * step:(b + 1) * step, :]
-        khatri = (var[:, None, :] * snap[None, :, :]).reshape(step * ns, rank)
-        hi, lo = split(khatri)
-        k3 = jnp.concatenate([hi, lo, hi], axis=1)
-        hi, lo = split(khatri.T)
-        kt3 = jnp.concatenate([hi, lo, hi], axis=1)
-        folded = jnp.zeros((step * ns, rank), f32)
+        k2, kt2 = khatri_ref[b], flipped_ref[b]
+        k3 = jnp.concatenate([k2, k2[:, :rank]], axis=1)
+        kt3 = jnp.concatenate([kt2, kt2[:, :n_rows]], axis=1)
+        folded = jnp.zeros((n_rows, rank), f32)
         for n in range(tiles):
+            if b == 0:
+                block = [part for g in range(n * per, (n + 1) * per) for part in sides(mine_ref[g], other_ref[g])]
+                block = jnp.concatenate(block, axis=0)
+                hi, lo = split(block)
+                down[n] = jnp.concatenate([hi, hi, lo], axis=0)
+                hi, lo = split(block.T)
+                across[n] = jnp.concatenate([hi, hi, lo], axis=0)
             model = dot(k3, across[n])
-            loads[b][n].wait()
-            hi, lo = split((model - data[b, n].reshape(step * ns, tile)) * lax.rsqrt(model))
+            data = data_ref[b * step:(b + 1) * step, :, n * tile:(n + 1) * tile].reshape(n_rows, tile)
+            hi, lo = split((model - data) * lax.rsqrt(model))
             folded = folded + dot(jnp.concatenate([hi, lo, hi], axis=1), down[n])
             part = dot(kt3, jnp.concatenate([hi, hi, lo], axis=0))
-            total[n] = part if b == 0 else total[n] + part
+            if b == 0:
+                total[n] = part
+            else:
+                block = (total[n] + part).T
+                for i in range(per):
+                    first, second = block[2 * i * own:(2 * i + 1) * own], block[(2 * i + 1) * own:(2 * i + 2) * own]
+                    kept_ref[n * per + i], given_ref[n * per + i] = sides(first, second)
         folded = folded.reshape(step, ns, rank)
-        sums = (folded * snap[None]).sum(1)
+        sums = (folded * snap_ref[...][None]).sum(1)
         kept_ref[groups, b * step:(b + 1) * step, :] = sums
         given_ref[groups, b * step:(b + 1) * step, :] = sums
-        snap_sum = snap_sum + (folded * var[:, None, :]).sum(0)
+        snap_sum = snap_sum + (folded * var_ref[b * step:(b + 1) * step, :][:, None, :]).sum(0)
     snaps_ref[...] = snap_sum
-    for n in range(tiles):
-        cells[n * tile:(n + 1) * tile, :] = total[n].T
-    for g in range(groups):
-        kept_ref[g] = cells[pl.ds(pl.multiple_of((2 * g + core) * own, own), own), :]
-        given_ref[g] = cells[pl.ds(pl.multiple_of((2 * g + 1 - core) * own, own), own), :]
-
-
-def contracted(core, tensor, mine, other, var, snap):
+
+
+def contracted(where, ready, mine, other):
     groups, own, rank = mine.shape
-    nv, ns, width = tensor.shape
-    blocks, tiles = 2, width // tile
+    nv, ns, width = ready[0].shape
+    tiles = width // tile
     halfsum = jax.ShapeDtypeStruct((groups + 1, own, rank), f32)
     return pl.pallas_call(
         contract,
         name="contract",
-        in_specs=[pl.BlockSpec(memory_space=pltpu.SMEM), hbm, vmem, vmem, hbm, hbm],
+        in_specs=[pl.BlockSpec(memory_space=pltpu.SMEM)] + [vmem] * 7,
         out_specs=[vmem] * 3,
         out_shape=[halfsum, halfsum, jax.ShapeDtypeStruct((ns, rank), f32)],
         scratch_shapes=[
-            pltpu.VMEM((blocks, tiles, nv // blocks, ns, tile), f32),
-            pltpu.VMEM((nv, rank), f32),
-            pltpu.VMEM((ns, rank), f32),
-            pltpu.VMEM((width, rank), f32),
             pltpu.VMEM((tiles, 3 * rank, tile), bf16),
             pltpu.VMEM((tiles, 3 * tile, rank), bf16),
             pltpu.VMEM((tiles, rank, tile), f32),
-            pltpu.SemaphoreType.DMA((blocks, tiles)),
-            pltpu.SemaphoreType.DMA((2,)),
         ],
-        compiler_params=pltpu.CompilerParams(vmem_limit_bytes=36 << 20),
+        compiler_params=pltpu.CompilerParams(vmem_limit_bytes=24 << 20),
         cost_estimate=pl.CostEstimate(
             flops=18 * nv * ns * width * rank, bytes_accessed=4 * nv * ns * width, transcendentals=nv * ns * width
         ),
-    )(core, hold(tensor), mine, other, hold(var), hold(snap))
+    )(where, *ready, mine, other)
 
 
 def turn(a, b):
@@ -151,7 +179,7 @@
     low = lax.broadcasted_iota(jnp.int32, (1, lanes), 1) < frag
     first = x_ref[1] == 0
     unit = lambda u: got_ref[pl.ds(u, n, stride=6), :]
-    sums = jnp.concatenate([unit(u).sum(0, keepdims=True) for u in range(4)], axis=0)
+    sums = got_ref[...].reshape(n // 4, 24, lanes).sum(0).reshape(4, 6, lanes).sum(0)[:4]
     cells = jnp.concatenate([pltpu.roll(sums, frag, 1), sums], axis=0)
     mixed = unit(4).reshape(16, n // 16, lanes)
     var, head = mixed.sum(0), mixed.sum(1)
@@ -188,9 +216,8 @@
     mine = lax.all_to_all(jnp.broadcast_to(cell_factor[None], (groups, *cell_factor.shape)), rows, 0, 0)
     other = lax.ppermute(mine, "core", swap)
     where = jnp.stack([lax.axis_index("core"), lax.axis_index("xh")])
-    kept, given, part_snaps = contracted(
-        where, tensor, mine, other, var_factor, snap_factor
-    )
+    ready = prepared(tensor, var_factor, snap_factor)
+    kept, given, part_snaps = contracted(where, ready, mine, other)
     got = lax.ppermute(given, "core", swap)
     sent = pl.pallas_call(
         pack, name="pack", in_specs=[vmem] * 3, out_specs=vmem,

time: 112 us -> 109 us (0.973)
  waiting for transfers between devices: 3.59 us -> 1.56 us
  Pallas kernels: 15 us -> 13.5 us
    pallas_call x1, Pallas kernels: 13.4 us -> 9.27 us  [contracted(): pl.pallas_call(contract, name='contract', in_specs=[pl.BlockSpec(memory_s...]
    pallas_call x0 -> x1, Pallas kernels: none -> 2.61 us  [prepared(): pl.pallas_call(prepare, name='prepare', in_specs=[hbm] * 3, out_specs=[vm...]
    ppermute x1, waiting for transfers between devices: 1.79 us -> 0.01 us  [local(): other = lax.ppermute(mine, 'core', swap)]
  transfers between devices with their start and end apart: 2 -> 2, of which waited for: 2 -> 1; matrix products, arithmetic and copies ran while one was open for 0% -> 0% of each run, Pallas kernels for 0% -> 2%
where the time goes in v4:
time: 109 us; the launch traced here: 108 us
  blocking collectives  86.6 us (79%)
  Pallas kernels  13.5 us (12%)
  starting transfers between devices  4.32 us (4%)
  waiting for transfers between devices  1.56 us (1%)
    all_to_all x2, blocking collectives, exchange(): lax.all_to_all(a.reshape(n, -1, 1, lanes), axes, 0, 0).reshape(-1, lanes)  62.2 us
    all_to_all x1, blocking collectives, local(): lax.all_to_all(jnp.broadcast_to(cell_factor[None], (groups, *cell_factor....  24.4 us
    pallas_call x1, Pallas kernels, contracted(): pl.pallas_call(contract, name='contract', in_specs=[pl.BlockSpec(memory_s...  9.27 us
    pallas_call x1, Pallas kernels, prepared(): pl.pallas_call(prepare, name='prepare', in_specs=[hbm] * 3, out_specs=[vm...  2.61 us
    ppermute x1, starting transfers between devices, local(): got = lax.ppermute(given, 'core', swap)  2.41 us
  transfers between devices with their start and end apart: 2, of which 1 were waited for; matrix products, arithmetic and copies ran while one was open for 0% of the time, Pallas kernels for 2%

profile of v4, /device:TPU:6, one launch (start us, length us, event | category | flops | bytes accessed | tf_op | source)
XLA Modules:
  0.0 107.6 jit_solution(8150986143816184544)
XLA Ops:
  0.6 0.8 broadcast_in_dim.2
  1.4 24.4 %all_to_all.15.mine_ref = f32[16,32,256]{2,1,0:T(8,128)S(1)} all-to-all(f32[16,32,256]{2,1,0:T(8,128)S(1)} %broadcast_in_dim.2), channel_id=1, replica_groups=mesh['xh'=2,'y'=8,'core'=2,'z'=8,'xl'=2] {'xh','y'}, dimensions={0} | all-to-all | bytes 1048576 | tf_op jit(solution)/shard_map/all_to_all | solution.py:216
  25.8 1.9 %collective-permute-start = (f32[16,32,256]{2,1,0:T(8,128)S(1)}, f32[16,32,256]{2,1,0:T(8,128)S(1)}, u32[]{:S(2)}, u32[]{:S(2)}) collective-permute-start(f32[16,32,256]{2,1,0:T(8,128)S(1)} %all_to_all.15.mine_ref), channel_id=1, source_target_pairs={{0,16},{16,0},{1,17},{17,1},{2,18},{18,2},{3,19},{19,3},{4,20},{20... | collective-permute-start | bytes 1572872 | tf_op jit(solution)/shard_map/ppermute | solution.py:217
  27.7 2.6 %prepare.1 = (f32[32,40,1024]{2,1,0:T(8,128)S(1)}, bf16[2,640,512]{2,1,0:T(8,128)(2,1)S(1)}, bf16[2,256,1280]{2,1,0:T(8,128)(2,1)S(1)}, f32[32,256]{1,0:T(8,128)S(1)}, f32[40,256]{1,0:T(8,128)S(1)}) custom-call(f32[32,40,1024]{2,1,0:T(8,128)} %tensor_hbm.1, f32[32,256]{1,0:T(8,128)} %var_hbm.1, f32[40,256]{1,0:T(8,128)} %snap_hbm.1), custom_call_target="tpu_custom_call" | custom-call | bytes 10485760 | tf_op jit(solution)/shard_map/prepare/pallas_call | solution.py:64
  30.3 0.1 pad_add_fusion.where_ref.x_ref
  30.4 0.0 collective-permute-done.other_ref
  30.4 9.3 %contract.1 = (f32[17,32,256]{2,1,0:T(8,128)S(1)}, f32[17,32,256]{2,1,0:T(8,128)S(1)}, f32[40,256]{1,0:T(8,128)S(1)}) custom-call(s32[2]{0:T(128)S(1)} %pad_add_fusion.where_ref.x_ref, f32[32,40,1024]{2,1,0:T(8,128)S(1)} %get-tuple-element.11.data_ref, bf16[2,640,512]{2,1,0:T(8,128)(2,1)S(1)} %get-tuple-element.12.khatri_ref, ...), custom_call_target="tpu_custom_call" | custom-call | flops 6039797760 | bytes 5242880 | tf_op jit(solution)/shard_map/contract/pallas_call | solution.py:132
  39.7 2.4 %collective-permute-start.1 = (f32[17,32,256]{2,1,0:T(8,128)S(1)}, f32[17,32,256]{2,1,0:T(8,128)S(1)}, u32[]{:S(2)}, u32[]{:S(2)}) collective-permute-start(f32[17,32,256]{2,1,0:T(8,128)S(1)} %get-tuple-element.17), channel_id=1, source_target_pairs={{0,16},{16,0},{1,17},{17,1},{2,18},{18,2},{3,19},{19,3},{4,20},{20... | collective-permute-start | bytes 1671176 | tf_op jit(solution)/shard_map/ppermute | solution.py:221
  42.1 1.6 %collective-permute-done.1.got_ref = f32[17,32,256]{2,1,0:T(8,128)S(1)} collective-permute-done((f32[17,32,256]{2,1,0:T(8,128)S(1)}, f32[17,32,256]{2,1,0:T(8,128)S(1)}, u32[]{:S(2)}, u32[]{:S(2)}) %collective-permute-start.1) | collective-permute-done | bytes 557088 | tf_op jit(solution)/shard_map/ppermute | solution.py:221
  43.7 0.2 pack.1
  43.9 43.6 %all_to_all.16 = f32[256,6,1,128]{3,2,1,0:T(1,128)S(1)} all-to-all(f32[256,6,1,128]{3,2,1,0:T(1,128)S(1)} %bitcast.9), channel_id=1, replica_groups=mesh['xh'=2,'y'=8,'core'=2,'z'=8,'xl'=2] {'xh','y','z','xl'}, dimensions={0} | all-to-all | bytes 1572864 | tf_op jit(solution)/shard_map/all_to_all | solution.py:210
  87.5 0.7 regroup.1
  88.2 18.6 %all_to_all.17 = f32[128,2,1,128]{3,1,2,0:T(2,128)S(1)} all-to-all(f32[128,2,1,128]{3,1,2,0:T(2,128)S(1)} %bitcast.10), channel_id=1, replica_groups=mesh['xh'=2,'y'=8,'core'=2,'z'=8,'xl'=2] {'y','z','xl'}, dimensions={0} | all-to-all | bytes 262144 | tf_op jit(solution)/shard_map/all_to_all | solution.py:210
  106.8 0.7 unpack.1
Async XLA Ops:
  25.8 4.6 %collective-permute-start = (f32[16,32,256]{2,1,0:T(8,128)S(1)}, f32[16,32,256]{2,1,0:T(8,128)S(1)}, u32[]{:S(2)}, u32[]{:S(2)}) collective-permute-start(f32[16,32,256]{2,1,0:T(8,128)S(1)} %all_to_all.15.mine_ref), channel_id=1, source_target_pairs={{0,16},{16,0},{1,17},{17,1},{2,18},{18,2},{3,19},{19,3},{4,20},{20... | collective-permute-start | bytes 1572872 | tf_op jit(solution)/shard_map/ppermute | solution.py:217
  39.7 4.0 %collective-permute-start.1 = (f32[17,32,256]{2,1,0:T(8,128)S(1)}, f32[17,32,256]{2,1,0:T(8,128)S(1)}, u32[]{:S(2)}, u32[]{:S(2)}) collective-permute-start(f32[17,32,256]{2,1,0:T(8,128)S(1)} %get-tuple-element.17), channel_id=1, source_target_pairs={{0,16},{16,0},{1,17},{17,1},{2,18},{18,2},{3,19},{19,3},{4,20},{20... | collective-permute-start | bytes 1671176 | tf_op jit(solution)/shard_map/ppermute | solution.py:221

commit v5 on v4

--- a/solution.py
+++ b/solution.py
@@ -10,7 +10,7 @@
 variables = ("z", "xl")
 swap = [(0, 1), (1, 0)]
 f32, bf16 = jnp.float32, jnp.bfloat16
-lanes, frag, tile = 128, 64, 256
+lanes, tile = 128, 256
 vmem = pl.BlockSpec(memory_space=pltpu.VMEM)
 hbm = pl.BlockSpec(memory_space=pltpu.HBM)
 small = pltpu.CompilerParams(vmem_limit_bytes=8 << 20)
@@ -147,49 +147,44 @@
     )(where, *ready, mine, other)
 
 
-def turn(a, b):
-    low = lax.broadcasted_iota(jnp.int32, a.shape, a.ndim - 1) < frag
-    axis = a.ndim - 1
-    return jnp.where(low, a, pltpu.roll(b, frag, axis)), jnp.where(low, pltpu.roll(a, frag, axis), b)
+units = 19
 
 
 def pack(kept_ref, got_ref, snaps_ref, out_ref):
     own, rank = kept_ref.shape[1:]
     ns = snaps_ref.shape[0]
-    n = out_ref.shape[0] // 6
-    zero = jnp.zeros((own, lanes), f32)
-
-    def put(x, h, u, a, b):
-        for i, block in enumerate(turn(a, b)):
-            out_ref[pl.ds((x * n // 2 + (2 * h + i) * own) * 6 + u, own, stride=6), :] = block
-
     for h in range(rank // lanes):
         side = slice(h * lanes, (h + 1) * lanes)
-        total = lambda g: kept_ref[g, :, side] + got_ref[g, :, side]
-        rest = jnp.concatenate([snaps_ref[own:, side], zero[: 2 * own - ns]], axis=0)
-        for x in range(2):
-            for u in range(4):
-                put(x, h, u, total(8 * x + u), total(8 * x + 4 + u))
-            put(x, h, 4, total(16), snaps_ref[:own, side])
-            put(x, h, 5, rest, zero)
-
-
-def regroup(x_ref, got_ref, out_ref):
-    n = got_ref.shape[0] // 6
-    low = lax.broadcasted_iota(jnp.int32, (1, lanes), 1) < frag
-    first = x_ref[1] == 0
-    unit = lambda u: got_ref[pl.ds(u, n, stride=6), :]
-    sums = got_ref[...].reshape(n // 4, 24, lanes).sum(0).reshape(4, 6, lanes).sum(0)[:4]
-    cells = jnp.concatenate([pltpu.roll(sums, frag, 1), sums], axis=0)
-    mixed = unit(4).reshape(16, n // 16, lanes)
-    var, head = mixed.sum(0), mixed.sum(1)
-    rest = unit(5).reshape(16, n // 16, lanes).sum(1)
-    snap = jnp.where(low, rest, head)
-    snap = jnp.where(first, snap[:8], snap[8:])
-    shape = (8, n // 16, lanes)
-    out = jnp.where(low[None], var[None], cells[:, None, :])
-    out_ref[pl.ds(0, n // 2, stride=2), :] = out.reshape(n // 2, lanes)
-    out_ref[pl.ds(1, n // 2, stride=2), :] = jnp.broadcast_to(snap[:, None, :], shape).reshape(n // 2, lanes)
+        rest = jnp.concatenate([snaps_ref[own:, side], jnp.zeros((2 * own - ns, lanes), f32)], axis=0)
+        for u in range(units):
+            if u < 17:
+                block = kept_ref[u, :, side] + got_ref[u, :, side]
+            else:
+                block = snaps_ref[:own, side] if u == 17 else rest
+            out_ref[pl.ds(h * own * units + u, own, stride=units), :] = block
+
+
+def regroup(got_ref, out_ref):
+    n = got_ref.shape[0] // units
+    unit = lambda u: got_ref[pl.ds(u, n, stride=units), :]
+    cells = jnp.concatenate([unit(u).sum(0, keepdims=True) for u in range(16)], axis=0)
+    grid = lambda u: unit(u).reshape(8, 8, lanes)
+    rest = jnp.concatenate([grid(16).sum(0), grid(17).sum(1), grid(18).sum(1)], axis=0)
+    for x in range(4):
+        out_ref[x, :8, :] = cells[8 * (x // 2):8 * (x // 2) + 8]
+        out_ref[x, 8:, :] = rest
+
+
+def combine(where_ref, got_ref, out_ref):
+    n = out_ref.shape[0] // 4
+    high, low = where_ref[1] == 0, where_ref[2] == 0
+    part = lambda x, i, k: got_ref[x, 8 * i:8 * (i + k), :]
+    cells = part(0, 0, 1) + part(1, 0, 1) + part(2, 0, 1) + part(3, 0, 1)
+    var = jnp.where(low, part(0, 1, 1) + part(2, 1, 1), part(1, 1, 1) + part(3, 1, 1))
+    snap = jnp.where(high, part(0, 2, 2) + part(1, 2, 2), part(2, 2, 2) + part(3, 2, 2))
+    shape = (8, 8, lanes)
+    for u, rows_of in enumerate([cells[:, None], var[None], snap[:8][:, None], snap[8:][:, None]]):
+        out_ref[pl.ds(u, n, stride=4), :] = jnp.broadcast_to(rows_of, shape).reshape(n, lanes)
 
 
 def unpack(got_ref, cells_ref, var_ref, snap_ref):
@@ -197,13 +192,14 @@
     ns = snap_ref.shape[0]
     for h in range(2):
         side = slice(h * lanes, (h + 1) * lanes)
-        part = lambda i, u: got_ref[pl.ds(2 * (2 * h + i) * own + u, own, stride=2), :]
-        var, cells = turn(part(0, 0), part(1, 0))
-        rest, first = turn(part(0, 1), part(1, 1))
-        var_ref[:, side] = var
-        snap_ref[:own, side] = first
-        snap_ref[own:, side] = rest[: ns - own]
-        cells_ref[:, side] = cells
+        part = lambda u, k: got_ref[pl.ds(4 * h * own + u, k, stride=4), :]
+        cells_ref[:, side] = part(0, own)
+        var_ref[:, side] = part(1, own)
+        snap_ref[:own, side] = part(2, own)
+        snap_ref[own:, side] = part(3, ns - own)
+
+
+plane = ("y", "z")
 
 
 def exchange(a, n, axes):
@@ -211,26 +207,32 @@
 
 
 def local(tensor, cell_factor, var_factor, snap_factor):
-    groups, peers = lax.axis_size(rows), lax.axis_size(variables)
-    n = groups * peers
+    groups, n = lax.axis_size(rows), lax.axis_size(plane)
     mine = lax.all_to_all(jnp.broadcast_to(cell_factor[None], (groups, *cell_factor.shape)), rows, 0, 0)
     other = lax.ppermute(mine, "core", swap)
-    where = jnp.stack([lax.axis_index("core"), lax.axis_index("xh")])
+    where = jnp.stack([lax.axis_index("core"), lax.axis_index("xh"), lax.axis_index("xl")])
     ready = prepared(tensor, var_factor, snap_factor)
     kept, given, part_snaps = contracted(where, ready, mine, other)
     got = lax.ppermute(given, "core", swap)
-    sent = pl.pallas_call(
-        pack, name="pack", in_specs=[vmem] * 3, out_specs=vmem,
-        out_shape=jax.ShapeDtypeStruct((6 * n, lanes), f32), compiler_params=small,
-    )(kept, got, part_snaps)
-    sent = pl.pallas_call(
-        regroup, name="regroup", in_specs=[pl.BlockSpec(memory_space=pltpu.SMEM), vmem], out_specs=vmem,
-        out_shape=jax.ShapeDtypeStruct((n, lanes), f32), compiler_params=small,
-    )(where, exchange(sent, n, rows + variables))
-    return pl.pallas_call(
-        unpack, name="unpack", in_specs=[vmem], out_specs=[vmem] * 3,
-        out_shape=[jax.ShapeDtypeStruct(a.shape, f32) for a in (cell_factor, var_factor, snap_factor)], compiler_params=small,
-    )(exchange(sent, n // 2, ("y",) + variables))
+
+    def call(kernel, shapes, *args):
+        scalars = sum(a.dtype == jnp.int32 for a in args)
+        return pl.pallas_call(
+            kernel,
+            name=kernel.__name__,
+            in_specs=[pl.BlockSpec(memory_space=pltpu.SMEM)] * scalars + [vmem] * (len(args) - scalars),
+            out_specs=[vmem] * len(shapes),
+            out_shape=[jax.ShapeDtypeStruct(shape, f32) for shape in shapes],
+            compiler_params=small,
+        )(*args)
+
+    (sent,) = call(pack, [(units * n, lanes)], kept, got, part_snaps)
+    (sent,) = call(regroup, [(4, 32, lanes)], exchange(sent, n, plane))
+    sent = lax.all_to_all(sent, ("xh", "xl"), 0, 0)
+    (sent,) = call(combine, [(4 * n, lanes)], where, sent)
+    return tuple(
+        call(unpack, [a.shape for a in (cell_factor, var_factor, snap_factor)], exchange(sent, n, plane))
+    )
 
 
 def solution(mesh):

time: 109 us -> 108 us (level)
    all_to_all x2, blocking collectives: 62.2 us -> 53.4 us  [exchange(): lax.all_to_all(a.reshape(n, -1, 1, lanes), axes, 0, 0).reshape(-1, lanes)]
    all_to_all x0 -> x1, blocking collectives: none -> 8.51 us  [local(): sent = lax.all_to_all(sent, ('xh', 'xl'), 0, 0)]
where the time goes in v5:
time: 108 us; the launch traced here: 107 us
  blocking collectives  86.3 us (80%)
  Pallas kernels  13.2 us (12%)
  starting transfers between devices  4.31 us (4%)
  waiting for transfers between devices  1.56 us (1%)
    all_to_all x2, blocking collectives, exchange(): lax.all_to_all(a.reshape(n, -1, 1, lanes), axes, 0, 0).reshape(-1, lanes)  53.4 us
    all_to_all x1, blocking collectives, local(): lax.all_to_all(jnp.broadcast_to(cell_factor[None], (groups, *cell_factor....  24.4 us
    pallas_call x1, Pallas kernels, contracted(): pl.pallas_call(contract, name='contract', in_specs=[pl.BlockSpec(memory_s...  9.27 us
    all_to_all x1, blocking collectives, local(): sent = lax.all_to_all(sent, ('xh', 'xl'), 0, 0)  8.51 us
    pallas_call x1, Pallas kernels, prepared(): pl.pallas_call(prepare, name='prepare', in_specs=[hbm] * 3, out_specs=[vm...  2.61 us
    ppermute x1, starting transfers between devices, local(): got = lax.ppermute(given, 'core', swap)  2.4 us
  transfers between devices with their start and end apart: 2, of which 1 were waited for; matrix products, arithmetic and copies ran while one was open for 0% of the time, Pallas kernels for 2%

profile of v5, /device:TPU:6, one launch (start us, length us, event | category | flops | bytes accessed | tf_op | source)
XLA Modules:
  0.0 107.0 jit_solution(11590988410219569808)
XLA Ops:
  0.6 0.8 broadcast_in_dim.2
  1.4 24.4 %all_to_all.20.mine_ref = f32[16,32,256]{2,1,0:T(8,128)S(1)} all-to-all(f32[16,32,256]{2,1,0:T(8,128)S(1)} %broadcast_in_dim.2), channel_id=1, replica_groups=mesh['xh'=2,'y'=8,'core'=2,'z'=8,'xl'=2] {'xh','y'}, dimensions={0} | all-to-all | bytes 1048576 | tf_op jit(solution)/shard_map/all_to_all | solution.py:211
  25.8 1.9 %collective-permute-start = (f32[16,32,256]{2,1,0:T(8,128)S(1)}, f32[16,32,256]{2,1,0:T(8,128)S(1)}, u32[]{:S(2)}, u32[]{:S(2)}) collective-permute-start(f32[16,32,256]{2,1,0:T(8,128)S(1)} %all_to_all.20.mine_ref), channel_id=1, source_target_pairs={{0,16},{16,0},{1,17},{17,1},{2,18},{18,2},{3,19},{19,3},{4,20},{20... | collective-permute-start | bytes 1572872 | tf_op jit(solution)/shard_map/ppermute | solution.py:212
  27.7 2.6 %prepare.1 = (f32[32,40,1024]{2,1,0:T(8,128)S(1)}, bf16[2,640,512]{2,1,0:T(8,128)(2,1)S(1)}, bf16[2,256,1280]{2,1,0:T(8,128)(2,1)S(1)}, f32[32,256]{1,0:T(8,128)S(1)}, f32[40,256]{1,0:T(8,128)S(1)}) custom-call(f32[32,40,1024]{2,1,0:T(8,128)} %tensor_hbm.1, f32[32,256]{1,0:T(8,128)} %var_hbm.1, f32[40,256]{1,0:T(8,128)} %snap_hbm.1), custom_call_target="tpu_custom_call" | custom-call | bytes 10485760 | tf_op jit(solution)/shard_map/prepare/pallas_call | solution.py:64
  30.3 0.1 pad_add_fusion.where_ref
  30.4 0.0 collective-permute-done.other_ref
  30.4 9.3 %contract.1 = (f32[17,32,256]{2,1,0:T(8,128)S(1)}, f32[17,32,256]{2,1,0:T(8,128)S(1)}, f32[40,256]{1,0:T(8,128)S(1)}) custom-call(s32[3]{0:T(128)S(1)} %pad_add_fusion.where_ref, f32[32,40,1024]{2,1,0:T(8,128)S(1)} %get-tuple-element.11.data_ref, bf16[2,640,512]{2,1,0:T(8,128)(2,1)S(1)} %get-tuple-element.12.khatri_ref, ...), custom_call_target="tpu_custom_call" | custom-call | flops 6039797760 | bytes 5242880 | tf_op jit(solution)/shard_map/contract/pallas_call | solution.py:132
  39.7 2.4 %collective-permute-start.1 = (f32[17,32,256]{2,1,0:T(8,128)S(1)}, f32[17,32,256]{2,1,0:T(8,128)S(1)}, u32[]{:S(2)}, u32[]{:S(2)}) collective-permute-start(f32[17,32,256]{2,1,0:T(8,128)S(1)} %get-tuple-element.17), channel_id=1, source_target_pairs={{0,16},{16,0},{1,17},{17,1},{2,18},{18,2},{3,19},{19,3},{4,20},{20... | collective-permute-start | bytes 1671176 | tf_op jit(solution)/shard_map/ppermute | solution.py:216
  42.1 1.6 %collective-permute-done.1.got_ref = f32[17,32,256]{2,1,0:T(8,128)S(1)} collective-permute-done((f32[17,32,256]{2,1,0:T(8,128)S(1)}, f32[17,32,256]{2,1,0:T(8,128)S(1)}, u32[]{:S(2)}, u32[]{:S(2)}) %collective-permute-start.1) | collective-permute-done | bytes 557088 | tf_op jit(solution)/shard_map/ppermute | solution.py:216
  43.7 0.1 pack.1
  43.8 34.5 %all_to_all.21 = f32[64,19,1,128]{3,2,1,0:T(1,128)S(1)} all-to-all(f32[64,19,1,128]{3,2,1,0:T(1,128)S(1)} %bitcast.9), channel_id=1, replica_groups=mesh['xh'=2,'y'=8,'core'=2,'z'=8,'xl'=2] {'y','z'}, dimensions={0} | all-to-all | bytes 1245184 | tf_op jit(solution)/shard_map/all_to_all | solution.py:206
  78.2 0.1 regroup.1
  78.3 8.5 %all_to_all.22.got_ref = f32[4,32,128]{2,1,0:T(8,128)S(1)} all-to-all(f32[4,32,128]{2,1,0:T(8,128)S(1)} %regroup.1), channel_id=1, replica_groups=mesh['xh'=2,'y'=8,'core'=2,'z'=8,'xl'=2] {'xh','xl'}, dimensions={0} | all-to-all | bytes 131072 | tf_op jit(solution)/shard_map/all_to_all | solution.py:231
  86.8 0.6 combine.1
  87.4 19.0 %all_to_all.23 = f32[64,4,1,128]{3,1,2,0:T(4,128)S(1)} all-to-all(f32[64,4,1,128]{3,1,2,0:T(4,128)S(1)} %bitcast.12), channel_id=1, replica_groups=mesh['xh'=2,'y'=8,'core'=2,'z'=8,'xl'=2] {'y','z'}, dimensions={0} | all-to-all | bytes 262144 | tf_op jit(solution)/shard_map/all_to_all | solution.py:206
  106.3 0.6 unpack.1
Async XLA Ops:
  25.8 4.6 %collective-permute-start = (f32[16,32,256]{2,1,0:T(8,128)S(1)}, f32[16,32,256]{2,1,0:T(8,128)S(1)}, u32[]{:S(2)}, u32[]{:S(2)}) collective-permute-start(f32[16,32,256]{2,1,0:T(8,128)S(1)} %all_to_all.20.mine_ref), channel_id=1, source_target_pairs={{0,16},{16,0},{1,17},{17,1},{2,18},{18,2},{3,19},{19,3},{4,20},{20... | collective-permute-start | bytes 1572872 | tf_op jit(solution)/shard_map/ppermute | solution.py:212
  39.7 4.0 %collective-permute-start.1 = (f32[17,32,256]{2,1,0:T(8,128)S(1)}, f32[17,32,256]{2,1,0:T(8,128)S(1)}, u32[]{:S(2)}, u32[]{:S(2)}) collective-permute-start(f32[17,32,256]{2,1,0:T(8,128)S(1)} %get-tuple-element.17), channel_id=1, source_target_pairs={{0,16},{16,0},{1,17},{17,1},{2,18},{18,2},{3,19},{19,3},{4,20},{20... | collective-permute-start | bytes 1671176 | tf_op jit(solution)/shard_map/ppermute | solution.py:216

commit v6 on v5

--- a/solution.py
+++ b/solution.py
@@ -29,17 +29,14 @@
     return jnp.dot(a, b, preferred_element_type=f32)
 
 
-def prepare(tensor_hbm, var_hbm, snap_hbm, data_ref, khatri_ref, flipped_ref, var_ref, snap_ref, sems, small_sems):
+def prepare(tensor_hbm, var_hbm, snap_hbm, data_ref, khatri_ref, flipped_ref, var_ref, snap_ref, sem, small_sems):
     blocks, n_rows, rank = khatri_ref.shape[0], khatri_ref.shape[1], khatri_ref.shape[2] // 2
-    step = data_ref.shape[0] // blocks
+    step = data_ref.shape[0]
     factors = [
         pltpu.make_async_copy(snap_hbm, snap_ref, small_sems.at[0]),
         pltpu.make_async_copy(var_hbm, var_ref, small_sems.at[1]),
     ]
-    loads = [
-        pltpu.make_async_copy(tensor_hbm.at[pl.ds(b * step, step)], data_ref.at[pl.ds(b * step, step)], sems.at[b])
-        for b in range(blocks)
-    ]
+    loads = [pltpu.make_async_copy(tensor_hbm.at[pl.ds(0, step)], data_ref, sem)]
     for copy in factors + loads:
         copy.start()
     for copy in factors:
@@ -67,31 +64,36 @@
         in_specs=[hbm] * 3,
         out_specs=[vmem] * 5,
         out_shape=[
-            jax.ShapeDtypeStruct(tensor.shape, f32),
+            jax.ShapeDtypeStruct((nv // blocks, ns, width), f32),
             jax.ShapeDtypeStruct((blocks, nv * ns // blocks, 2 * rank), bf16),
             jax.ShapeDtypeStruct((blocks, rank, 2 * nv * ns // blocks), bf16),
             jax.ShapeDtypeStruct(var.shape, f32),
             jax.ShapeDtypeStruct(snap.shape, f32),
         ],
-        scratch_shapes=[pltpu.SemaphoreType.DMA((blocks,)), pltpu.SemaphoreType.DMA((2,))],
+        scratch_shapes=[pltpu.SemaphoreType.DMA(()), pltpu.SemaphoreType.DMA((2,))],
         compiler_params=small,
         cost_estimate=pl.CostEstimate(flops=0, bytes_accessed=8 * nv * ns * width, transcendentals=0),
     )(hold(tensor), hold(var), hold(snap))
 
 
-def contract(where_ref, data_ref, khatri_ref, flipped_ref, var_ref, snap_ref, mine_ref, other_ref,
-             kept_ref, given_ref, snaps_ref, across, down, total):
+def contract(tensor_hbm, data_ref, khatri_ref, flipped_ref, var_ref, snap_ref, mine_ref, other_ref,
+             kept_ref, given_ref, snaps_ref, late_ref, across, down, total, sem):
     groups, own, rank = mine_ref.shape
-    nv, ns, width = data_ref.shape
+    step, ns, width = data_ref.shape
     blocks, n_rows = khatri_ref.shape[:2]
-    tiles, step, per = width // tile, nv // blocks, tile // own // 2
-    even = where_ref[0] == 0
+    tiles, per = width // tile, tile // own // 2
+    even = lax.axis_index("core") == 0
 
     def sides(a, b):
         return jnp.where(even, a, b), jnp.where(even, b, a)
 
+    load = pltpu.make_async_copy(tensor_hbm.at[pl.ds(step, step)], late_ref, sem)
+    load.start()
     snap_sum = jnp.zeros((ns, rank), f32)
     for b in range(blocks):
+        if b == 1:
+            load.wait()
+        source = data_ref if b == 0 else late_ref
         k2, kt2 = khatri_ref[b], flipped_ref[b]
         k3 = jnp.concatenate([k2, k2[:, :rank]], axis=1)
         kt3 = jnp.concatenate([kt2, kt2[:, :n_rows]], axis=1)
@@ -105,7 +107,7 @@
                 hi, lo = split(block.T)
                 across[n] = jnp.concatenate([hi, hi, lo], axis=0)
             model = dot(k3, across[n])
-            data = data_ref[b * step:(b + 1) * step, :, n * tile:(n + 1) * tile].reshape(n_rows, tile)
+            data = source[:, :, n * tile:(n + 1) * tile].reshape(n_rows, tile)
             hi, lo = split((model - data) * lax.rsqrt(model))
             folded = folded + dot(jnp.concatenate([hi, lo, hi], axis=1), down[n])
             part = dot(kt3, jnp.concatenate([hi, hi, lo], axis=0))
@@ -124,27 +126,29 @@
     snaps_ref[...] = snap_sum
 
 
-def contracted(where, ready, mine, other):
+def contracted(tensor, ready, mine, other):
     groups, own, rank = mine.shape
-    nv, ns, width = ready[0].shape
+    nv, ns, width = tensor.shape
     tiles = width // tile
     halfsum = jax.ShapeDtypeStruct((groups + 1, own, rank), f32)
     return pl.pallas_call(
         contract,
         name="contract",
-        in_specs=[pl.BlockSpec(memory_space=pltpu.SMEM)] + [vmem] * 7,
+        in_specs=[hbm] + [vmem] * 7,
         out_specs=[vmem] * 3,
         out_shape=[halfsum, halfsum, jax.ShapeDtypeStruct((ns, rank), f32)],
         scratch_shapes=[
+            pltpu.VMEM((nv // 2, ns, width), f32),
             pltpu.VMEM((tiles, 3 * rank, tile), bf16),
             pltpu.VMEM((tiles, 3 * tile, rank), bf16),
             pltpu.VMEM((tiles, rank, tile), f32),
+            pltpu.SemaphoreType.DMA(()),
         ],
         compiler_params=pltpu.CompilerParams(vmem_limit_bytes=24 << 20),
         cost_estimate=pl.CostEstimate(
             flops=18 * nv * ns * width * rank, bytes_accessed=4 * nv * ns * width, transcendentals=nv * ns * width
         ),
-    )(where, *ready, mine, other)
+    )(hold(tensor), *ready, mine, other)
 
 
 units = 19
@@ -175,16 +179,22 @@
         out_ref[x, 8:, :] = rest
 
 
-def combine(where_ref, got_ref, out_ref):
-    n = out_ref.shape[0] // 4
-    high, low = where_ref[1] == 0, where_ref[2] == 0
+def combine(got_ref, out_ref):
+    high, low = lax.axis_index("xh") == 0, lax.axis_index("xl") == 0
     part = lambda x, i, k: got_ref[x, 8 * i:8 * (i + k), :]
     cells = part(0, 0, 1) + part(1, 0, 1) + part(2, 0, 1) + part(3, 0, 1)
     var = jnp.where(low, part(0, 1, 1) + part(2, 1, 1), part(1, 1, 1) + part(3, 1, 1))
     snap = jnp.where(high, part(0, 2, 2) + part(1, 2, 2), part(2, 2, 2) + part(3, 2, 2))
     shape = (8, 8, lanes)
-    for u, rows_of in enumerate([cells[:, None], var[None], snap[:8][:, None], snap[8:][:, None]]):
-        out_ref[pl.ds(u, n, stride=4), :] = jnp.broadcast_to(rows_of, shape).reshape(n, lanes)
+    line = lax.broadcasted_iota(jnp.int32, shape, 1)
+    each = lambda a: jnp.broadcast_to(a[:, None], shape)
+    base = jnp.where(line % 4 == 0, each(cells), jnp.where(line % 4 == 2, each(snap[:8]), each(snap[8:])))
+    var = each(var)
+    for k in range(4):
+        pair = jnp.where(line[0] < 4, var[2 * k], var[2 * k + 1])
+        block = jnp.where(line % 4 == 1, pair[None], base)
+        for y in range(8):
+            out_ref[32 * y + 8 * k:32 * y + 8 * k + 8, :] = block[y]
 
 
 def unpack(got_ref, cells_ref, var_ref, snap_ref):
@@ -210,17 +220,15 @@
     groups, n = lax.axis_size(rows), lax.axis_size(plane)
     mine = lax.all_to_all(jnp.broadcast_to(cell_factor[None], (groups, *cell_factor.shape)), rows, 0, 0)
     other = lax.ppermute(mine, "core", swap)
-    where = jnp.stack([lax.axis_index("core"), lax.axis_index("xh"), lax.axis_index("xl")])
     ready = prepared(tensor, var_factor, snap_factor)
-    kept, given, part_snaps = contracted(where, ready, mine, other)
+    kept, given, part_snaps = contracted(tensor, ready, mine, other)
     got = lax.ppermute(given, "core", swap)
 
     def call(kernel, shapes, *args):
-        scalars = sum(a.dtype == jnp.int32 for a in args)
         return pl.pallas_call(
             kernel,
             name=kernel.__name__,
-            in_specs=[pl.BlockSpec(memory_space=pltpu.SMEM)] * scalars + [vmem] * (len(args) - scalars),
+            in_specs=[vmem] * len(args),
             out_specs=[vmem] * len(shapes),
             out_shape=[jax.ShapeDtypeStruct(shape, f32) for shape in shapes],
             compiler_params=small,
@@ -229,7 +237,7 @@
     (sent,) = call(pack, [(units * n, lanes)], kept, got, part_snaps)
     (sent,) = call(regroup, [(4, 32, lanes)], exchange(sent, n, plane))
     sent = lax.all_to_all(sent, ("xh", "xl"), 0, 0)
-    (sent,) = call(combine, [(4 * n, lanes)], where, sent)
+    (sent,) = call(combine, [(4 * n, lanes)], sent)
     return tuple(
         call(unpack, [a.shape for a in (cell_factor, var_factor, snap_factor)], exchange(sent, n, plane))
     )

time: 108 us -> 106 us (0.981)
  Pallas kernels: 13.2 us -> 11.6 us
  transfers between devices with their start and end apart: 2 -> 2, of which waited for: 1 -> 2; matrix products, arithmetic and copies ran while one was open for 0% -> 0% of each run, Pallas kernels for 2% -> 2%
where the time goes in v6:
time: 106 us; the launch traced here: 105 us
  blocking collectives  86.3 us (81%)
  Pallas kernels  11.6 us (11%)
  starting transfers between devices  4.28 us (4%)
  waiting for transfers between devices  1.62 us (2%)
    all_to_all x2, blocking collectives, exchange(): lax.all_to_all(a.reshape(n, -1, 1, lanes), axes, 0, 0).reshape(-1, lanes)  53.4 us
    all_to_all x1, blocking collectives, local(): lax.all_to_all(jnp.broadcast_to(cell_factor[None], (groups, *cell_factor....  24.4 us
    pallas_call x1, Pallas kernels, contracted(): pl.pallas_call(contract, name='contract', in_specs=[hbm] + [vmem] * 7, ou...  8.93 us
    all_to_all x1, blocking collectives, local(): sent = lax.all_to_all(sent, ('xh', 'xl'), 0, 0)  8.51 us
    ppermute x1, starting transfers between devices, local(): got = lax.ppermute(given, 'core', swap)  2.37 us
  transfers between devices with their start and end apart: 2, of which 2 were waited for; matrix products, arithmetic and copies ran while one was open for 0% of the time, Pallas kernels for 2%

profile of v6, /device:TPU:6, one launch (start us, length us, event | category | flops | bytes accessed | tf_op | source)
XLA Modules:
  0.0 105.2 jit_solution(3369556593324761934)
XLA Ops:
  0.6 0.8 broadcast_in_dim.2
  1.4 24.4 %all_to_all.20.mine_ref = f32[16,32,256]{2,1,0:T(8,128)S(1)} all-to-all(f32[16,32,256]{2,1,0:T(8,128)S(1)} %broadcast_in_dim.2), channel_id=1, replica_groups=mesh['xh'=2,'y'=8,'core'=2,'z'=8,'xl'=2] {'xh','y'}, dimensions={0} | all-to-all | bytes 1048576 | tf_op jit(solution)/shard_map/all_to_all | solution.py:221
  25.8 1.9 %collective-permute-start = (f32[16,32,256]{2,1,0:T(8,128)S(1)}, f32[16,32,256]{2,1,0:T(8,128)S(1)}, u32[]{:S(2)}, u32[]{:S(2)}) collective-permute-start(f32[16,32,256]{2,1,0:T(8,128)S(1)} %all_to_all.20.mine_ref), channel_id=1, source_target_pairs={{0,16},{16,0},{1,17},{17,1},{2,18},{18,2},{3,19},{19,3},{4,20},{20... | collective-permute-start | bytes 1572872 | tf_op jit(solution)/shard_map/ppermute | solution.py:222
  27.7 1.8 %prepare.1 = (f32[16,40,1024]{2,1,0:T(8,128)S(1)}, bf16[2,640,512]{2,1,0:T(8,128)(2,1)S(1)}, bf16[2,256,1280]{2,1,0:T(8,128)(2,1)S(1)}, f32[32,256]{1,0:T(8,128)S(1)}, f32[40,256]{1,0:T(8,128)S(1)}) custom-call(f32[32,40,1024]{2,1,0:T(8,128)} %tensor_hbm.3, f32[32,256]{1,0:T(8,128)} %var_hbm.1, f32[40,256]{1,0:T(8,128)} %snap_hbm.1), custom_call_target="tpu_custom_call" | custom-call | bytes 10485760 | tf_op jit(solution)/shard_map/prepare/pallas_call | solution.py:61
  29.5 0.1 collective-permute-done.other_ref
  29.6 8.9 %contract.1 = (f32[17,32,256]{2,1,0:T(8,128)S(1)}, f32[17,32,256]{2,1,0:T(8,128)S(1)}, f32[40,256]{1,0:T(8,128)S(1)}) custom-call(f32[32,40,1024]{2,1,0:T(8,128)} %tensor_hbm.3, f32[16,40,1024]{2,1,0:T(8,128)S(1)} %get-tuple-element.11.data_ref, bf16[2,640,512]{2,1,0:T(8,128)(2,1)S(1)} %get-tuple-element.12.khatri_ref, ...), custom_call_target="tpu_custom_call" | custom-call | flops 6039797760 | bytes 5242880 | tf_op jit(solution)/shard_map/contract/pallas_call | solution.py:134
  38.5 2.4 %collective-permute-start.1 = (f32[17,32,256]{2,1,0:T(8,128)S(1)}, f32[17,32,256]{2,1,0:T(8,128)S(1)}, u32[]{:S(2)}, u32[]{:S(2)}) collective-permute-start(f32[17,32,256]{2,1,0:T(8,128)S(1)} %get-tuple-element.17), channel_id=1, source_target_pairs={{0,16},{16,0},{1,17},{17,1},{2,18},{18,2},{3,19},{19,3},{4,20},{20... | collective-permute-start | bytes 1671176 | tf_op jit(solution)/shard_map/ppermute | solution.py:225
  40.9 1.6 %collective-permute-done.1.got_ref = f32[17,32,256]{2,1,0:T(8,128)S(1)} collective-permute-done((f32[17,32,256]{2,1,0:T(8,128)S(1)}, f32[17,32,256]{2,1,0:T(8,128)S(1)}, u32[]{:S(2)}, u32[]{:S(2)}) %collective-permute-start.1) | collective-permute-done | bytes 557088 | tf_op jit(solution)/shard_map/ppermute | solution.py:225
  42.5 0.1 pack.1
  42.5 34.5 %all_to_all.21 = f32[64,19,1,128]{3,2,1,0:T(1,128)S(1)} all-to-all(f32[64,19,1,128]{3,2,1,0:T(1,128)S(1)} %bitcast.6), channel_id=1, replica_groups=mesh['xh'=2,'y'=8,'core'=2,'z'=8,'xl'=2] {'y','z'}, dimensions={0} | all-to-all | bytes 1245184 | tf_op jit(solution)/shard_map/all_to_all | solution.py:216
  77.0 0.1 regroup.1
  77.1 8.5 %all_to_all.22.got_ref = f32[4,32,128]{2,1,0:T(8,128)S(1)} all-to-all(f32[4,32,128]{2,1,0:T(8,128)S(1)} %regroup.1), channel_id=1, replica_groups=mesh['xh'=2,'y'=8,'core'=2,'z'=8,'xl'=2] {'xh','xl'}, dimensions={0} | all-to-all | bytes 131072 | tf_op jit(solution)/shard_map/all_to_all | solution.py:239
  85.6 19.0 %all_to_all.23 = f32[64,4,1,128]{3,1,2,0:T(4,128)S(1)} all-to-all(f32[64,4,1,128]{3,1,2,0:T(4,128)S(1)} %bitcast.9), channel_id=1, replica_groups=mesh['xh'=2,'y'=8,'core'=2,'z'=8,'xl'=2] {'y','z'}, dimensions={0} | all-to-all | bytes 262144 | tf_op jit(solution)/shard_map/all_to_all | solution.py:216
  104.6 0.6 unpack.1
  (1 shorter events, 0.0 us)
Async XLA Ops:
  25.8 3.8 %collective-permute-start = (f32[16,32,256]{2,1,0:T(8,128)S(1)}, f32[16,32,256]{2,1,0:T(8,128)S(1)}, u32[]{:S(2)}, u32[]{:S(2)}) collective-permute-start(f32[16,32,256]{2,1,0:T(8,128)S(1)} %all_to_all.20.mine_ref), channel_id=1, source_target_pairs={{0,16},{16,0},{1,17},{17,1},{2,18},{18,2},{3,19},{19,3},{4,20},{20... | collective-permute-start | bytes 1572872 | tf_op jit(solution)/shard_map/ppermute | solution.py:222
  38.5 3.9 %collective-permute-start.1 = (f32[17,32,256]{2,1,0:T(8,128)S(1)}, f32[17,32,256]{2,1,0:T(8,128)S(1)}, u32[]{:S(2)}, u32[]{:S(2)}) collective-permute-start(f32[17,32,256]{2,1,0:T(8,128)S(1)} %get-tuple-element.17), channel_id=1, source_target_pairs={{0,16},{16,0},{1,17},{17,1},{2,18},{18,2},{3,19},{19,3},{4,20},{20... | collective-permute-start | bytes 1671176 | tf_op jit(solution)/shard_map/ppermute | solution.py:225

commit v7 on v6

--- a/solution.py
+++ b/solution.py
@@ -1,3 +1,5 @@
+import functools
+
 import jax
 import jax.numpy as jnp
 from jax import lax
@@ -5,8 +7,8 @@
 from jax.experimental.pallas import tpu as pltpu
 from jax.sharding import Mesh, PartitionSpec as P
 
+
 snaps = ("xh", "y", "core")
-rows = ("xh", "y")
 variables = ("z", "xl")
 swap = [(0, 1), (1, 0)]
 f32, bf16 = jnp.float32, jnp.bfloat16
@@ -76,39 +78,55 @@
     )(hold(tensor), hold(var), hold(snap))
 
 
-def contract(tensor_hbm, data_ref, khatri_ref, flipped_ref, var_ref, snap_ref, mine_ref, other_ref,
-             kept_ref, given_ref, snaps_ref, late_ref, across, down, total, sem):
-    groups, own, rank = mine_ref.shape
+def contract(stage, tensor_hbm, data_ref, khatri_ref, flipped_ref, var_ref, snap_ref, mine_ref, other_ref, *refs):
+    own, rank = mine_ref.shape[1:]
     step, ns, width = data_ref.shape
     blocks, n_rows = khatri_ref.shape[:2]
-    tiles, per = width // tile, tile // own // 2
-    even = lax.axis_index("core") == 0
+    half = width // 2
+    tiles, per = half // tile // (2 - stage // 2), tile // own // 2
+    skip = per * tiles if stage == 1 else 0
+    if stage > 0:
+        before_ref, *refs = refs
+    if stage == 2:
+        early, refs = refs[:2], refs[2:]
+    kept_ref, given_ref, last_ref, late_ref, across, down, total, sem = refs
+    even, x = lax.axis_index("core") == 0, lax.axis_index("xh")
+    start = (x if stage < 2 else 1 - x) * half + (tile if stage == 1 else 0)
 
     def sides(a, b):
         return jnp.where(even, a, b), jnp.where(even, b, a)
 
-    load = pltpu.make_async_copy(tensor_hbm.at[pl.ds(step, step)], late_ref, sem)
+    columns = pl.ds(pl.multiple_of(start, tile), tiles * tile)
+    load = pltpu.make_async_copy(tensor_hbm.at[pl.ds(step, step), :, columns], late_ref, sem)
     load.start()
+    shift = 0
+    if stage == 2:
+        shift = 2 * early[0].shape[0]
+        for i, ref in enumerate(early):
+            given_ref[i * ref.shape[0]:(i + 1) * ref.shape[0]] = ref[...]
     snap_sum = jnp.zeros((ns, rank), f32)
     for b in range(blocks):
         if b == 1:
             load.wait()
-        source = data_ref if b == 0 else late_ref
         k2, kt2 = khatri_ref[b], flipped_ref[b]
         k3 = jnp.concatenate([k2, k2[:, :rank]], axis=1)
         kt3 = jnp.concatenate([kt2, kt2[:, :n_rows]], axis=1)
-        folded = jnp.zeros((n_rows, rank), f32)
+        folded = before_ref[b] if stage > 0 else jnp.zeros((n_rows, rank), f32)
         for n in range(tiles):
             if b == 0:
-                block = [part for g in range(n * per, (n + 1) * per) for part in sides(mine_ref[g], other_ref[g])]
+                near = range(skip + n * per, skip + (n + 1) * per)
+                block = [part for g in near for part in sides(mine_ref[g], other_ref[g])]
                 block = jnp.concatenate(block, axis=0)
                 hi, lo = split(block)
                 down[n] = jnp.concatenate([hi, hi, lo], axis=0)
                 hi, lo = split(block.T)
                 across[n] = jnp.concatenate([hi, hi, lo], axis=0)
             model = dot(k3, across[n])
-            data = source[:, :, n * tile:(n + 1) * tile].reshape(n_rows, tile)
-            hi, lo = split((model - data) * lax.rsqrt(model))
+            if b == 0:
+                data = data_ref[:, :, pl.ds(pl.multiple_of(start + n * tile, tile), tile)]
+            else:
+                data = late_ref[:, :, n * tile:(n + 1) * tile]
+            hi, lo = split((model - data.reshape(n_rows, tile)) * lax.rsqrt(model))
             folded = folded + dot(jnp.concatenate([hi, lo, hi], axis=1), down[n])
             part = dot(kt3, jnp.concatenate([hi, hi, lo], axis=0))
             if b == 0:
@@ -117,52 +135,60 @@
                 block = (total[n] + part).T
                 for i in range(per):
                     first, second = block[2 * i * own:(2 * i + 1) * own], block[(2 * i + 1) * own:(2 * i + 2) * own]
-                    kept_ref[n * per + i], given_ref[n * per + i] = sides(first, second)
+                    kept_ref[n * per + i], given_ref[shift + n * per + i] = sides(first, second)
+        if stage < 2:
+            last_ref[b] = folded
+            continue
         folded = folded.reshape(step, ns, rank)
         sums = (folded * snap_ref[...][None]).sum(1)
-        kept_ref[groups, b * step:(b + 1) * step, :] = sums
-        given_ref[groups, b * step:(b + 1) * step, :] = sums
+        kept_ref[tiles * per, b * step:(b + 1) * step, :] = sums
+        given_ref[shift + tiles * per, b * step:(b + 1) * step, :] = sums
         snap_sum = snap_sum + (folded * var_ref[b * step:(b + 1) * step, :][:, None, :]).sum(0)
-    snaps_ref[...] = snap_sum
-
-
-def contracted(tensor, ready, mine, other):
+    if stage == 2:
+        last_ref[...] = snap_sum
+
+
+def contracted(stage, tensor, ready, mine, other, *more):
     groups, own, rank = mine.shape
     nv, ns, width = tensor.shape
-    tiles = width // tile
-    halfsum = jax.ShapeDtypeStruct((groups + 1, own, rank), f32)
+    tiles = width // 2 // tile // (2 - stage // 2)
+    shape = lambda *a: jax.ShapeDtypeStruct(a, f32)
+    if stage < 2:
+        outs = [shape(groups // 2, own, rank), shape(groups // 2, own, rank), shape(2, nv * ns // 2, rank)]
+    else:
+        outs = [shape(groups + 1, own, rank), shape(2 * groups + 1, own, rank), shape(ns, rank)]
+    work = nv * ns * tiles * tile
     return pl.pallas_call(
-        contract,
+        functools.partial(contract, stage),
         name="contract",
-        in_specs=[hbm] + [vmem] * 7,
+        in_specs=[hbm] + [vmem] * (7 + len(more)),
         out_specs=[vmem] * 3,
-        out_shape=[halfsum, halfsum, jax.ShapeDtypeStruct((ns, rank), f32)],
+        out_shape=outs,
         scratch_shapes=[
-            pltpu.VMEM((nv // 2, ns, width), f32),
+            pltpu.VMEM((nv // 2, ns, tiles * tile), f32),
             pltpu.VMEM((tiles, 3 * rank, tile), bf16),
             pltpu.VMEM((tiles, 3 * tile, rank), bf16),
             pltpu.VMEM((tiles, rank, tile), f32),
             pltpu.SemaphoreType.DMA(()),
         ],
         compiler_params=pltpu.CompilerParams(vmem_limit_bytes=24 << 20),
-        cost_estimate=pl.CostEstimate(
-            flops=18 * nv * ns * width * rank, bytes_accessed=4 * nv * ns * width, transcendentals=nv * ns * width
-        ),
-    )(hold(tensor), *ready, mine, other)
+        cost_estimate=pl.CostEstimate(flops=18 * work * rank, bytes_accessed=4 * work, transcendentals=work),
+    )(hold(tensor), *ready, mine, other, *more)
 
 
 units = 19
 
 
-def pack(kept_ref, got_ref, snaps_ref, out_ref):
-    own, rank = kept_ref.shape[1:]
+def pack(first_ref, second_ref, third_ref, got_ref, snaps_ref, out_ref):
+    own, rank = first_ref.shape[1:]
+    kept = [(ref, i) for ref in (first_ref, second_ref, third_ref) for i in range(ref.shape[0])]
     ns = snaps_ref.shape[0]
     for h in range(rank // lanes):
         side = slice(h * lanes, (h + 1) * lanes)
         rest = jnp.concatenate([snaps_ref[own:, side], jnp.zeros((2 * own - ns, lanes), f32)], axis=0)
         for u in range(units):
             if u < 17:
-                block = kept_ref[u, :, side] + got_ref[u, :, side]
+                block = kept[u][0][kept[u][1], :, side] + got_ref[u, :, side]
             else:
                 block = snaps_ref[:own, side] if u == 17 else rest
             out_ref[pl.ds(h * own * units + u, own, stride=units), :] = block
@@ -175,7 +201,7 @@
     grid = lambda u: unit(u).reshape(8, 8, lanes)
     rest = jnp.concatenate([grid(16).sum(0), grid(17).sum(1), grid(18).sum(1)], axis=0)
     for x in range(4):
-        out_ref[x, :8, :] = cells[8 * (x // 2):8 * (x // 2) + 8]
+        out_ref[x, :8, :] = jnp.where(lax.axis_index("xh") == x // 2, cells[:8], cells[8:])
         out_ref[x, 8:, :] = rest
 
 
@@ -217,24 +243,27 @@
 
 
 def local(tensor, cell_factor, var_factor, snap_factor):
-    groups, n = lax.axis_size(rows), lax.axis_size(plane)
-    mine = lax.all_to_all(jnp.broadcast_to(cell_factor[None], (groups, *cell_factor.shape)), rows, 0, 0)
+    near, n = lax.axis_size("y"), lax.axis_size(plane)
+    mine = lax.all_to_all(jnp.broadcast_to(cell_factor[None], (near, *cell_factor.shape)), "y", 0, 0)
+    far = lax.ppermute(mine, ("xh", "xl"), [(0, 3), (3, 0), (1, 2), (2, 1)])
     other = lax.ppermute(mine, "core", swap)
     ready = prepared(tensor, var_factor, snap_factor)
-    kept, given, part_snaps = contracted(tensor, ready, mine, other)
+    kept0, given0, folded = contracted(0, tensor, ready, mine, other)
+    far_other = lax.ppermute(far, "core", swap)
+    kept1, given1, folded = contracted(1, tensor, ready, mine, other, folded)
+    kept2, given, part_snaps = contracted(2, tensor, ready, far, far_other, folded, given0, given1)
     got = lax.ppermute(given, "core", swap)
 
     def call(kernel, shapes, *args):
         return pl.pallas_call(
             kernel,
-            name=kernel.__name__,
             in_specs=[vmem] * len(args),
             out_specs=[vmem] * len(shapes),
             out_shape=[jax.ShapeDtypeStruct(shape, f32) for shape in shapes],
             compiler_params=small,
         )(*args)
 
-    (sent,) = call(pack, [(units * n, lanes)], kept, got, part_snaps)
+    (sent,) = call(pack, [(units * n, lanes)], kept0, kept1, kept2, got, part_snaps)
     (sent,) = call(regroup, [(4, 32, lanes)], exchange(sent, n, plane))
     sent = lax.all_to_all(sent, ("xh", "xl"), 0, 0)
     (sent,) = call(combine, [(4 * n, lanes)], sent)

time: 106 us -> 108 us (1.019)
  blocking collectives: 86.3 us -> 78.7 us
  starting transfers between devices: 4.28 us -> 8.61 us
  waiting for transfers between devices: 1.62 us -> 4.91 us
  Pallas kernels: 11.6 us -> 12.9 us
    all_to_all x1, blocking collectives: 24.4 us -> 18.8 us  [local(): lax.all_to_all(jnp.broadcast_to(cell_factor[None], (near, *cell_factor.sh...]
    ppermute x0 -> x2, starting transfers between devices: none -> 4.28 us  [the longest x1 2.37 us: local(): far = lax.ppermute(mine, ('xh', 'xl'), [(0, 3), (3, 0), (1, 2), (2, 1)])]
    ppermute x0 -> x2, waiting for transfers between devices: none -> 3.35 us  [the longest x1 3.35 us: local(): far = lax.ppermute(mine, ('xh', 'xl'), [(0, 3), (3, 0), (1, 2), (2, 1)])]
    all_to_all x2, blocking collectives: 53.4 us -> 52 us  [exchange(): lax.all_to_all(a.reshape(n, -1, 1, lanes), axes, 0, 0).reshape(-1, lanes)]
    pallas_call x5 -> x7, Pallas kernels: 9.74 us -> 11.1 us  [the longest x3 10.3 us: contracted(): pl.pallas_call(functools.partial(contract, stage), name='contract', in_sp...]
  transfers between devices with their start and end apart: 2 -> 4, of which waited for: 2 -> 2; matrix products, arithmetic and copies ran while one was open for 0% -> 0% of each run, Pallas kernels for 2% -> 6%
where the time goes in v7:
time: 108 us; the launch traced here: 107 us
  blocking collectives  78.7 us (73%)
  Pallas kernels  12.9 us (12%)
  starting transfers between devices  8.61 us (8%)
  waiting for transfers between devices  4.91 us (5%)
    all_to_all x2, blocking collectives, exchange(): lax.all_to_all(a.reshape(n, -1, 1, lanes), axes, 0, 0).reshape(-1, lanes)  52 us
    all_to_all x1, blocking collectives, local(): lax.all_to_all(jnp.broadcast_to(cell_factor[None], (near, *cell_factor.sh...  18.8 us
    pallas_call x3, Pallas kernels, contracted(): pl.pallas_call(functools.partial(contract, stage), name='contract', in_sp...  10.3 us
    all_to_all x1, blocking collectives, local(): sent = lax.all_to_all(sent, ('xh', 'xl'), 0, 0)  7.86 us
    ppermute x1, waiting for transfers between devices, local(): far = lax.ppermute(mine, ('xh', 'xl'), [(0, 3), (3, 0), (1, 2), (2, 1)])  3.35 us
    ppermute x1, starting transfers between devices, local(): got = lax.ppermute(given, 'core', swap)  2.4 us
    ppermute x1, starting transfers between devices, local(): far = lax.ppermute(mine, ('xh', 'xl'), [(0, 3), (3, 0), (1, 2), (2, 1)])  2.37 us
  transfers between devices with their start and end apart: 4, of which 2 were waited for; matrix products, arithmetic and copies ran while one was open for 0% of the time, Pallas kernels for 6%

profile of v7, /device:TPU:6, one launch (start us, length us, event | category | flops | bytes accessed | tf_op | source)
XLA Modules:
  0.0 106.6 jit_solution(16930860084741979843)
XLA Ops:
  0.6 0.8 broadcast_in_dim.2
  1.4 18.8 %all_to_all.20.mine_ref = f32[8,32,256]{2,1,0:T(8,128)S(1)} all-to-all(f32[8,32,256]{2,1,0:T(8,128)S(1)} %broadcast_in_dim.2), channel_id=1, replica_groups=mesh['xh'=2,'y'=8,'core'=2,'z'=8,'xl'=2] {'y'}, dimensions={0} | all-to-all | bytes 524288 | tf_op jit(solution)/shard_map/all_to_all | solution.py:247
  20.2 2.4 %collective-permute-start.1 = (f32[8,32,256]{2,1,0:T(8,128)S(1)}, f32[8,32,256]{2,1,0:T(8,128)S(1)}, u32[]{:S(2)}, u32[]{:S(2)}) collective-permute-start(f32[8,32,256]{2,1,0:T(8,128)S(1)} %all_to_all.20.mine_ref), channel_id=1, source_target_pairs={{0,257},{257,0},{1,256},{256,1},{2,259},{259,2},{3,258},{258,3},{4... | collective-permute-start | bytes 786440 | tf_op jit(solution)/shard_map/ppermute | solution.py:248
  22.6 1.9 %collective-permute-start = (f32[8,32,256]{2,1,0:T(8,128)S(1)}, f32[8,32,256]{2,1,0:T(8,128)S(1)}, u32[]{:S(2)}, u32[]{:S(2)}) collective-permute-start(f32[8,32,256]{2,1,0:T(8,128)S(1)} %all_to_all.20.mine_ref), channel_id=1, source_target_pairs={{0,16},{16,0},{1,17},{17,1},{2,18},{18,2},{3,19},{19,3},{4,20},{20... | collective-permute-start | bytes 786440 | tf_op jit(solution)/shard_map/ppermute | solution.py:249
  24.5 1.8 %prepare.1 = (f32[16,40,1024]{2,1,0:T(8,128)S(1)}, bf16[2,640,512]{2,1,0:T(8,128)(2,1)S(1)}, bf16[2,256,1280]{2,1,0:T(8,128)(2,1)S(1)}, f32[32,256]{1,0:T(8,128)S(1)}, f32[40,256]{1,0:T(8,128)S(1)}) custom-call(f32[32,40,1024]{2,1,0:T(8,128)} %tensor_hbm.7, f32[32,256]{1,0:T(8,128)} %var_hbm.1, f32[40,256]{1,0:T(8,128)} %snap_hbm.1), custom_call_target="tpu_custom_call" | custom-call | bytes 10485760 | tf_op jit(solution)/shard_map/prepare/pallas_call | solution.py:63
  26.3 3.3 %collective-permute-done.1.mine_ref = f32[8,32,256]{2,1,0:T(8,128)S(1)} collective-permute-done((f32[8,32,256]{2,1,0:T(8,128)S(1)}, f32[8,32,256]{2,1,0:T(8,128)S(1)}, u32[]{:S(2)}, u32[]{:S(2)}) %collective-permute-start.1) | collective-permute-done | bytes 262176 | tf_op jit(solution)/shard_map/ppermute | solution.py:248
  29.7 1.9 %collective-permute-start.2 = (f32[8,32,256]{2,1,0:T(8,128)S(1)}, f32[8,32,256]{2,1,0:T(8,128)S(1)}, u32[]{:S(2)}, u32[]{:S(2)}) collective-permute-start(f32[8,32,256]{2,1,0:T(8,128)S(1)} %collective-permute-done.1.mine_ref), channel_id=1, source_target_pairs={{0,16},{16,0},{1,17},{17,1},{2,18},{18,2},{3,19},{19,3},{4,20},{20... | collective-permute-start | bytes 786440 | tf_op jit(solution)/shard_map/ppermute | solution.py:252
  31.6 0.0 collective-permute-done.other_ref
  31.6 2.5 %contract.3 = (f32[4,32,256]{2,1,0:T(8,128)S(1)}, f32[4,32,256]{2,1,0:T(8,128)S(1)}, f32[2,640,256]{2,1,0:T(8,128)S(1)}) custom-call(f32[32,40,1024]{2,1,0:T(8,128)} %tensor_hbm.7, f32[16,40,1024]{2,1,0:T(8,128)S(1)} %get-tuple-element.17.data_ref, bf16[2,640,512]{2,1,0:T(8,128)(2,1)S(1)} %get-tuple-element.18.khatri_ref, ...), custom_call_target="tpu_custom_call" | custom-call | flops 1509949440 | bytes 1310720 | tf_op jit(solution)/shard_map/contract/pallas_call | solution.py:161
  34.1 2.5 %contract.4 = (f32[4,32,256]{2,1,0:T(8,128)S(1)}, f32[4,32,256]{2,1,0:T(8,128)S(1)}, f32[2,640,256]{2,1,0:T(8,128)S(1)}) custom-call(f32[32,40,1024]{2,1,0:T(8,128)} %tensor_hbm.7, f32[16,40,1024]{2,1,0:T(8,128)S(1)} %get-tuple-element.17.data_ref, bf16[2,640,512]{2,1,0:T(8,128)(2,1)S(1)} %get-tuple-element.18.khatri_ref, ...), custom_call_target="tpu_custom_call" | custom-call | flops 1509949440 | bytes 1310720 | tf_op jit(solution)/shard_map/contract/pallas_call | solution.py:161
  36.7 0.0 collective-permute-done.2.other_ref
  36.7 5.2 %contract.5 = (f32[9,32,256]{2,1,0:T(8,128)S(1)}, f32[17,32,256]{2,1,0:T(8,128)S(1)}, f32[40,256]{1,0:T(8,128)S(1)}) custom-call(f32[32,40,1024]{2,1,0:T(8,128)} %tensor_hbm.7, f32[16,40,1024]{2,1,0:T(8,128)S(1)} %get-tuple-element.17.data_ref, bf16[2,640,512]{2,1,0:T(8,128)(2,1)S(1)} %get-tuple-element.18.khatri_ref, ...), custom_call_target="tpu_custom_call" | custom-call | flops 3019898880 | bytes 2621440 | tf_op jit(solution)/shard_map/contract/pallas_call | solution.py:161
  41.9 2.4 %collective-permute-start.3 = (f32[17,32,256]{2,1,0:T(8,128)S(1)}, f32[17,32,256]{2,1,0:T(8,128)S(1)}, u32[]{:S(2)}, u32[]{:S(2)}) collective-permute-start(f32[17,32,256]{2,1,0:T(8,128)S(1)} %get-tuple-element.29), channel_id=1, source_target_pairs={{0,16},{16,0},{1,17},{17,1},{2,18},{18,2},{3,19},{19,3},{4,20},{20... | collective-permute-start | bytes 1671176 | tf_op jit(solution)/shard_map/ppermute | solution.py:255
  44.3 1.6 %collective-permute-done.3.got_ref = f32[17,32,256]{2,1,0:T(8,128)S(1)} collective-permute-done((f32[17,32,256]{2,1,0:T(8,128)S(1)}, f32[17,32,256]{2,1,0:T(8,128)S(1)}, u32[]{:S(2)}, u32[]{:S(2)}) %collective-permute-start.3) | collective-permute-done | bytes 557088 | tf_op jit(solution)/shard_map/ppermute | solution.py:255
  45.9 0.1 shard_map.67
  46.0 33.2 %all_to_all.21 = f32[64,19,1,128]{3,2,1,0:T(1,128)S(1)} all-to-all(f32[64,19,1,128]{3,2,1,0:T(1,128)S(1)} %bitcast.6), channel_id=1, replica_groups=mesh['xh'=2,'y'=8,'core'=2,'z'=8,'xl'=2] {'y','z'}, dimensions={0} | all-to-all | bytes 1245184 | tf_op jit(solution)/shard_map/all_to_all | solution.py:242
  79.1 0.1 shard_map.68
  79.2 7.9 %all_to_all.22.got_ref = f32[4,32,128]{2,1,0:T(8,128)S(1)} all-to-all(f32[4,32,128]{2,1,0:T(8,128)S(1)} %shard_map.68), channel_id=1, replica_groups=mesh['xh'=2,'y'=8,'core'=2,'z'=8,'xl'=2] {'xh','xl'}, dimensions={0} | all-to-all | bytes 131072 | tf_op jit(solution)/shard_map/all_to_all | solution.py:268
  87.1 18.9 %all_to_all.23 = f32[64,4,1,128]{3,1,2,0:T(4,128)S(1)} all-to-all(f32[64,4,1,128]{3,1,2,0:T(4,128)S(1)} %bitcast.9), channel_id=1, replica_groups=mesh['xh'=2,'y'=8,'core'=2,'z'=8,'xl'=2] {'y','z'}, dimensions={0} | all-to-all | bytes 262144 | tf_op jit(solution)/shard_map/all_to_all | solution.py:242
  106.0 0.6 shard_map.70
  (1 shorter events, 0.0 us)
Async XLA Ops:
  20.2 9.5 %collective-permute-start.1 = (f32[8,32,256]{2,1,0:T(8,128)S(1)}, f32[8,32,256]{2,1,0:T(8,128)S(1)}, u32[]{:S(2)}, u32[]{:S(2)}) collective-permute-start(f32[8,32,256]{2,1,0:T(8,128)S(1)} %all_to_all.20.mine_ref), channel_id=1, source_target_pairs={{0,257},{257,0},{1,256},{256,1},{2,259},{259,2},{3,258},{258,3},{4... | collective-permute-start | bytes 786440 | tf_op jit(solution)/shard_map/ppermute | solution.py:248
  22.6 9.0 %collective-permute-start = (f32[8,32,256]{2,1,0:T(8,128)S(1)}, f32[8,32,256]{2,1,0:T(8,128)S(1)}, u32[]{:S(2)}, u32[]{:S(2)}) collective-permute-start(f32[8,32,256]{2,1,0:T(8,128)S(1)} %all_to_all.20.mine_ref), channel_id=1, source_target_pairs={{0,16},{16,0},{1,17},{17,1},{2,18},{18,2},{3,19},{19,3},{4,20},{20... | collective-permute-start | bytes 786440 | tf_op jit(solution)/shard_map/ppermute | solution.py:249
  29.7 7.0 %collective-permute-start.2 = (f32[8,32,256]{2,1,0:T(8,128)S(1)}, f32[8,32,256]{2,1,0:T(8,128)S(1)}, u32[]{:S(2)}, u32[]{:S(2)}) collective-permute-start(f32[8,32,256]{2,1,0:T(8,128)S(1)} %collective-permute-done.1.mine_ref), channel_id=1, source_target_pairs={{0,16},{16,0},{1,17},{17,1},{2,18},{18,2},{3,19},{19,3},{4,20},{20... | collective-permute-start | bytes 786440 | tf_op jit(solution)/shard_map/ppermute | solution.py:252
  41.9 4.0 %collective-permute-start.3 = (f32[17,32,256]{2,1,0:T(8,128)S(1)}, f32[17,32,256]{2,1,0:T(8,128)S(1)}, u32[]{:S(2)}, u32[]{:S(2)}) collective-permute-start(f32[17,32,256]{2,1,0:T(8,128)S(1)} %get-tuple-element.29), channel_id=1, source_target_pairs={{0,16},{16,0},{1,17},{17,1},{2,18},{18,2},{3,19},{19,3},{4,20},{20... | collective-permute-start | bytes 1671176 | tf_op jit(solution)/shard_map/ppermute | solution.py:255

commit v8 on v7

--- a/solution.py
+++ b/solution.py
@@ -119,9 +119,15 @@
                 block = jnp.concatenate(block, axis=0)
                 hi, lo = split(block)
                 down[n] = jnp.concatenate([hi, hi, lo], axis=0)
-                hi, lo = split(block.T)
-                across[n] = jnp.concatenate([hi, hi, lo], axis=0)
-            model = dot(k3, across[n])
+                if stage == 2:
+                    across[n] = jnp.concatenate([hi, hi, lo], axis=1)
+                else:
+                    hi, lo = split(block.T)
+                    across[n] = jnp.concatenate([hi, hi, lo], axis=0)
+            if stage == 2:
+                model = lax.dot_general(k3, across[n], (((1,), (1,)), ((), ())), preferred_element_type=f32)
+            else:
+                model = dot(k3, across[n])
             if b == 0:
                 data = data_ref[:, :, pl.ds(pl.multiple_of(start + n * tile, tile), tile)]
             else:
@@ -166,7 +172,7 @@
         out_shape=outs,
         scratch_shapes=[
             pltpu.VMEM((nv // 2, ns, tiles * tile), f32),
-            pltpu.VMEM((tiles, 3 * rank, tile), bf16),
+            pltpu.VMEM((tiles, tile, 3 * rank) if stage == 2 else (tiles, 3 * rank, tile), bf16),
             pltpu.VMEM((tiles, 3 * tile, rank), bf16),
             pltpu.VMEM((tiles, rank, tile), f32),
             pltpu.SemaphoreType.DMA(()),

time: 108 us -> 109 us (level)
  no operation moved by 1% of the time
where the time goes in v8:
time: 109 us; the launch traced here: 108 us
  blocking collectives  78.7 us (72%)
  Pallas kernels  13.9 us (13%)
  starting transfers between devices  8.61 us (8%)
  waiting for transfers between devices  4.91 us (5%)
    all_to_all x2, blocking collectives, exchange(): lax.all_to_all(a.reshape(n, -1, 1, lanes), axes, 0, 0).reshape(-1, lanes)  52 us
    all_to_all x1, blocking collectives, local(): lax.all_to_all(jnp.broadcast_to(cell_factor[None], (near, *cell_factor.sh...  18.8 us
    pallas_call x3, Pallas kernels, contracted(): pl.pallas_call(functools.partial(contract, stage), name='contract', in_sp...  11.3 us
    all_to_all x1, blocking collectives, local(): sent = lax.all_to_all(sent, ('xh', 'xl'), 0, 0)  7.86 us
    ppermute x1, waiting for transfers between devices, local(): far = lax.ppermute(mine, ('xh', 'xl'), [(0, 3), (3, 0), (1, 2), (2, 1)])  3.35 us
    ppermute x1, starting transfers between devices, local(): got = lax.ppermute(given, 'core', swap)  2.41 us
    ppermute x1, starting transfers between devices, local(): far = lax.ppermute(mine, ('xh', 'xl'), [(0, 3), (3, 0), (1, 2), (2, 1)])  2.37 us
  transfers between devices with their start and end apart: 4, of which 2 were waited for; matrix products, arithmetic and copies ran while one was open for 0% of the time, Pallas kernels for 6%

profile of v8, /device:TPU:6, one launch (start us, length us, event | category | flops | bytes accessed | tf_op | source)
XLA Modules:
  0.0 107.6 jit_solution(13640668222762351210)
XLA Ops:
  0.6 0.8 broadcast_in_dim.2
  1.4 18.8 %all_to_all.20.mine_ref = f32[8,32,256]{2,1,0:T(8,128)S(1)} all-to-all(f32[8,32,256]{2,1,0:T(8,128)S(1)} %broadcast_in_dim.2), channel_id=1, replica_groups=mesh['xh'=2,'y'=8,'core'=2,'z'=8,'xl'=2] {'y'}, dimensions={0} | all-to-all | bytes 524288 | tf_op jit(solution)/shard_map/all_to_all | solution.py:253
  20.2 2.4 %collective-permute-start.1 = (f32[8,32,256]{2,1,0:T(8,128)S(1)}, f32[8,32,256]{2,1,0:T(8,128)S(1)}, u32[]{:S(2)}, u32[]{:S(2)}) collective-permute-start(f32[8,32,256]{2,1,0:T(8,128)S(1)} %all_to_all.20.mine_ref), channel_id=1, source_target_pairs={{0,257},{257,0},{1,256},{256,1},{2,259},{259,2},{3,258},{258,3},{4... | collective-permute-start | bytes 786440 | tf_op jit(solution)/shard_map/ppermute | solution.py:254
  22.6 1.9 %collective-permute-start = (f32[8,32,256]{2,1,0:T(8,128)S(1)}, f32[8,32,256]{2,1,0:T(8,128)S(1)}, u32[]{:S(2)}, u32[]{:S(2)}) collective-permute-start(f32[8,32,256]{2,1,0:T(8,128)S(1)} %all_to_all.20.mine_ref), channel_id=1, source_target_pairs={{0,16},{16,0},{1,17},{17,1},{2,18},{18,2},{3,19},{19,3},{4,20},{20... | collective-permute-start | bytes 786440 | tf_op jit(solution)/shard_map/ppermute | solution.py:255
  24.5 1.8 %prepare.1 = (f32[16,40,1024]{2,1,0:T(8,128)S(1)}, bf16[2,640,512]{2,1,0:T(8,128)(2,1)S(1)}, bf16[2,256,1280]{2,1,0:T(8,128)(2,1)S(1)}, f32[32,256]{1,0:T(8,128)S(1)}, f32[40,256]{1,0:T(8,128)S(1)}) custom-call(f32[32,40,1024]{2,1,0:T(8,128)} %tensor_hbm.7, f32[32,256]{1,0:T(8,128)} %var_hbm.1, f32[40,256]{1,0:T(8,128)} %snap_hbm.1), custom_call_target="tpu_custom_call" | custom-call | bytes 10485760 | tf_op jit(solution)/shard_map/prepare/pallas_call | solution.py:63
  26.3 3.3 %collective-permute-done.1.mine_ref = f32[8,32,256]{2,1,0:T(8,128)S(1)} collective-permute-done((f32[8,32,256]{2,1,0:T(8,128)S(1)}, f32[8,32,256]{2,1,0:T(8,128)S(1)}, u32[]{:S(2)}, u32[]{:S(2)}) %collective-permute-start.1) | collective-permute-done | bytes 262176 | tf_op jit(solution)/shard_map/ppermute | solution.py:254
  29.7 1.9 %collective-permute-start.2 = (f32[8,32,256]{2,1,0:T(8,128)S(1)}, f32[8,32,256]{2,1,0:T(8,128)S(1)}, u32[]{:S(2)}, u32[]{:S(2)}) collective-permute-start(f32[8,32,256]{2,1,0:T(8,128)S(1)} %collective-permute-done.1.mine_ref), channel_id=1, source_target_pairs={{0,16},{16,0},{1,17},{17,1},{2,18},{18,2},{3,19},{19,3},{4,20},{20... | collective-permute-start | bytes 786440 | tf_op jit(solution)/shard_map/ppermute | solution.py:258
  31.6 0.0 collective-permute-done.other_ref
  31.6 2.5 %contract.3 = (f32[4,32,256]{2,1,0:T(8,128)S(1)}, f32[4,32,256]{2,1,0:T(8,128)S(1)}, f32[2,640,256]{2,1,0:T(8,128)S(1)}) custom-call(f32[32,40,1024]{2,1,0:T(8,128)} %tensor_hbm.7, f32[16,40,1024]{2,1,0:T(8,128)S(1)} %get-tuple-element.17.data_ref, bf16[2,640,512]{2,1,0:T(8,128)(2,1)S(1)} %get-tuple-element.18.khatri_ref, ...), custom_call_target="tpu_custom_call" | custom-call | flops 1509949440 | bytes 1310720 | tf_op jit(solution)/shard_map/contract/pallas_call | solution.py:167
  34.1 2.5 %contract.4 = (f32[4,32,256]{2,1,0:T(8,128)S(1)}, f32[4,32,256]{2,1,0:T(8,128)S(1)}, f32[2,640,256]{2,1,0:T(8,128)S(1)}) custom-call(f32[32,40,1024]{2,1,0:T(8,128)} %tensor_hbm.7, f32[16,40,1024]{2,1,0:T(8,128)S(1)} %get-tuple-element.17.data_ref, bf16[2,640,512]{2,1,0:T(8,128)(2,1)S(1)} %get-tuple-element.18.khatri_ref, ...), custom_call_target="tpu_custom_call" | custom-call | flops 1509949440 | bytes 1310720 | tf_op jit(solution)/shard_map/contract/pallas_call | solution.py:167
  36.7 0.0 collective-permute-done.2.other_ref
  36.7 6.3 %contract.5 = (f32[9,32,256]{2,1,0:T(8,128)S(1)}, f32[17,32,256]{2,1,0:T(8,128)S(1)}, f32[40,256]{1,0:T(8,128)S(1)}) custom-call(f32[32,40,1024]{2,1,0:T(8,128)} %tensor_hbm.7, f32[16,40,1024]{2,1,0:T(8,128)S(1)} %get-tuple-element.17.data_ref, bf16[2,640,512]{2,1,0:T(8,128)(2,1)S(1)} %get-tuple-element.18.khatri_ref, ...), custom_call_target="tpu_custom_call" | custom-call | flops 3019898880 | bytes 2621440 | tf_op jit(solution)/shard_map/contract/pallas_call | solution.py:167
  42.9 2.4 %collective-permute-start.3 = (f32[17,32,256]{2,1,0:T(8,128)S(1)}, f32[17,32,256]{2,1,0:T(8,128)S(1)}, u32[]{:S(2)}, u32[]{:S(2)}) collective-permute-start(f32[17,32,256]{2,1,0:T(8,128)S(1)} %get-tuple-element.29), channel_id=1, source_target_pairs={{0,16},{16,0},{1,17},{17,1},{2,18},{18,2},{3,19},{19,3},{4,20},{20... | collective-permute-start | bytes 1671176 | tf_op jit(solution)/shard_map/ppermute | solution.py:261
  45.4 1.6 %collective-permute-done.3.got_ref = f32[17,32,256]{2,1,0:T(8,128)S(1)} collective-permute-done((f32[17,32,256]{2,1,0:T(8,128)S(1)}, f32[17,32,256]{2,1,0:T(8,128)S(1)}, u32[]{:S(2)}, u32[]{:S(2)}) %collective-permute-start.3) | collective-permute-done | bytes 557088 | tf_op jit(solution)/shard_map/ppermute | solution.py:261
  46.9 0.1 shard_map.67
  47.0 33.2 %all_to_all.21 = f32[64,19,1,128]{3,2,1,0:T(1,128)S(1)} all-to-all(f32[64,19,1,128]{3,2,1,0:T(1,128)S(1)} %bitcast.6), channel_id=1, replica_groups=mesh['xh'=2,'y'=8,'core'=2,'z'=8,'xl'=2] {'y','z'}, dimensions={0} | all-to-all | bytes 1245184 | tf_op jit(solution)/shard_map/all_to_all | solution.py:248
  80.2 0.1 shard_map.68
  80.2 7.9 %all_to_all.22.got_ref = f32[4,32,128]{2,1,0:T(8,128)S(1)} all-to-all(f32[4,32,128]{2,1,0:T(8,128)S(1)} %shard_map.68), channel_id=1, replica_groups=mesh['xh'=2,'y'=8,'core'=2,'z'=8,'xl'=2] {'xh','xl'}, dimensions={0} | all-to-all | bytes 131072 | tf_op jit(solution)/shard_map/all_to_all | solution.py:274
  88.1 18.9 %all_to_all.23 = f32[64,4,1,128]{3,1,2,0:T(4,128)S(1)} all-to-all(f32[64,4,1,128]{3,1,2,0:T(4,128)S(1)} %bitcast.9), channel_id=1, replica_groups=mesh['xh'=2,'y'=8,'core'=2,'z'=8,'xl'=2] {'y','z'}, dimensions={0} | all-to-all | bytes 262144 | tf_op jit(solution)/shard_map/all_to_all | solution.py:248
  107.0 0.6 shard_map.70
  (1 shorter events, 0.0 us)
Async XLA Ops:
  20.2 9.5 %collective-permute-start.1 = (f32[8,32,256]{2,1,0:T(8,128)S(1)}, f32[8,32,256]{2,1,0:T(8,128)S(1)}, u32[]{:S(2)}, u32[]{:S(2)}) collective-permute-start(f32[8,32,256]{2,1,0:T(8,128)S(1)} %all_to_all.20.mine_ref), channel_id=1, source_target_pairs={{0,257},{257,0},{1,256},{256,1},{2,259},{259,2},{3,258},{258,3},{4... | collective-permute-start | bytes 786440 | tf_op jit(solution)/shard_map/ppermute | solution.py:254
  22.6 9.0 %collective-permute-start = (f32[8,32,256]{2,1,0:T(8,128)S(1)}, f32[8,32,256]{2,1,0:T(8,128)S(1)}, u32[]{:S(2)}, u32[]{:S(2)}) collective-permute-start(f32[8,32,256]{2,1,0:T(8,128)S(1)} %all_to_all.20.mine_ref), channel_id=1, source_target_pairs={{0,16},{16,0},{1,17},{17,1},{2,18},{18,2},{3,19},{19,3},{4,20},{20... | collective-permute-start | bytes 786440 | tf_op jit(solution)/shard_map/ppermute | solution.py:255
  29.7 7.0 %collective-permute-start.2 = (f32[8,32,256]{2,1,0:T(8,128)S(1)}, f32[8,32,256]{2,1,0:T(8,128)S(1)}, u32[]{:S(2)}, u32[]{:S(2)}) collective-permute-start(f32[8,32,256]{2,1,0:T(8,128)S(1)} %collective-permute-done.1.mine_ref), channel_id=1, source_target_pairs={{0,16},{16,0},{1,17},{17,1},{2,18},{18,2},{3,19},{19,3},{4,20},{20... | collective-permute-start | bytes 786440 | tf_op jit(solution)/shard_map/ppermute | solution.py:258
  42.9 4.0 %collective-permute-start.3 = (f32[17,32,256]{2,1,0:T(8,128)S(1)}, f32[17,32,256]{2,1,0:T(8,128)S(1)}, u32[]{:S(2)}, u32[]{:S(2)}) collective-permute-start(f32[17,32,256]{2,1,0:T(8,128)S(1)} %get-tuple-element.29), channel_id=1, source_target_pairs={{0,16},{16,0},{1,17},{17,1},{2,18},{18,2},{3,19},{19,3},{4,20},{20... | collective-permute-start | bytes 1671176 | tf_op jit(solution)/shard_map/ppermute | solution.py:261
